TPU v7x, 32 devices: a whole 2x2x4 slice. The times are simulated.
32 devices in a mesh: context: 4 (over y, x), experts: 8 (over z, core).
Axes of the slice: x: 2, y: 2, z: 4, core: 2. Of those that a mesh axis runs over, the one named last changes fastest.
Arguments:
- inputs: bfloat16 [8, 512, 2048], P('experts', 'context'), may hold values from -6 to 6
- cotangent: bfloat16 [8, 512, 2048], P('experts', 'context'), may hold values from -6 to 6
- expert_ids: int32 [8, 512, 6], P('experts', 'context'), may hold values from 0 to 15, all different within a row; in each aligned block of 128 rows (0 to 127, 128 to 255, ..., all dimensions but the last counted through in order) at most 56 rows name the same one
- attn_gain: bfloat16 [2048], P(('context', 'experts')), may hold values from 0.5 to 1.5
- query_weight: bfloat16 [2048, 3072], P(('context', 'experts')), may hold values from -0.125 to 0.125
- latent_down: bfloat16 [2048, 576], P(('context', 'experts')), may hold values from -0.125 to 0.125
- latent_gain: bfloat16 [512], P(('context', 'experts')), may hold values from 0.5 to 1.5
- latent_up: bfloat16 [512, 4096], P(('context', 'experts')), may hold values from -0.25 to 0.25
- output_weight: bfloat16 [2048, 2048], P(('context', 'experts')), may hold values from -1.5 to 1.5
- ffn_gain: bfloat16 [2048], P(('context', 'experts')), may hold values from 0.5 to 1.5
- router_weight: bfloat16 [2048, 16], P(('context', 'experts')), may hold values from -0.0625 to 0.0625
- shared_gate: bfloat16 [2048, 2816], P(('context', 'experts')), may hold values from -0.125 to 0.125
- shared_up: bfloat16 [2048, 2816], P(('context', 'experts')), may hold values from -0.125 to 0.125
- shared_down: bfloat16 [2816, 2048], P(('context', 'experts')), may hold values from -0.109375 to 0.109375
- expert_gate: bfloat16 [16, 2048, 1408], P('experts', None, 'context'), may hold values from -0.125 to 0.125
- expert_up: bfloat16 [16, 2048, 1408], P('experts', None, 'context'), may hold values from -0.125 to 0.125
- expert_down: bfloat16 [16, 1408, 2048], P('experts', 'context'), may hold values from -6 to 6
Outputs:
- output: bfloat16 [8, 512, 2048], P('experts', 'context')
- inputs_grad: float32 [8, 512, 2048], P('experts', 'context')
- attn_gain_grad: float32 [2048], P(('context', 'experts'))
- query_weight_grad: float32 [2048, 3072], P(('context', 'experts'))
- latent_down_grad: float32 [2048, 576], P(('context', 'experts'))
- latent_gain_grad: float32 [512], P(('context', 'experts'))
- latent_up_grad: float32 [512, 4096], P(('context', 'experts'))
- output_weight_grad: float32 [2048, 2048], P(('context', 'experts'))
- ffn_gain_grad: float32 [2048], P(('context', 'experts'))
- router_weight_grad: float32 [2048, 16], P(('context', 'experts'))
- shared_gate_grad: float32 [2048, 2816], P(('context', 'experts'))
- shared_up_grad: float32 [2048, 2816], P(('context', 'experts'))
- shared_down_grad: float32 [2816, 2048], P(('context', 'experts'))
- expert_gate_grad: float32 [16, 2048, 1408], P('experts', None, 'context')
- expert_up_grad: float32 [16, 2048, 1408], P('experts', None, 'context')
- expert_down_grad: float32 [16, 1408, 2048], P('experts', 'context')
Inputs may be any that keep to these rules, and one draw needn't show every extreme that they name: `expert_ids`: each token names 6 different experts. Among the 128 tokens of one device no expert is named more than 56 times, and in some such block one expert is named exactly 56 times.
All inputs are finite; a program needn't handle non-finite values.
Results may differ from a plain program's by a relative error of at most 0.024.
Values may be sent and summed in bfloat16 or wider, within the bound.
No kernel may reach another device: no remote copies, remote signals or barrier semaphores. Data moves between devices by JAX's collectives and lax.ppermute only.
A program may use at most 448 MiB of HBM per device.

v0:
```python
import math

import jax
import jax.numpy as jnp
from jax import lax
from jax.sharding import Mesh
from jax.sharding import PartitionSpec as P


HEADS = 16
NOPE = 128
ROPE_D = 64
VD = 128
KVR = 512
P_DEV = 64
C_DEV = 64
EPS = 1e-06

CTX = "context"
EXP = ("chip", "core")
ALL = ("context", "chip", "core")
BF = jnp.bfloat16
F32 = jnp.float32


def mm(left, right):
    return lax.dot_general(left, right, (((1,), (0,)), ((), ())), preferred_element_type=F32)


def mm_tn(left, right):
    return lax.dot_general(left, right, (((0,), (0,)), ((), ())), preferred_element_type=F32)


def mm_nt(left, right):
    return lax.dot_general(left, right, (((1,), (1,)), ((), ())), preferred_element_type=F32)


def rotation(position, width):
    half = width // 2
    freqs = 10000.0 ** (-2.0 * jnp.arange(half).astype(F32) / width)
    angle = position.astype(F32)[:, None] * freqs[None, :]
    return (jnp.cos(angle), jnp.sin(angle))


def place_of(device, offset, prompt_total):
    return jnp.where(
        offset < P_DEV, device * P_DEV + offset, prompt_total + device * C_DEV + offset - P_DEV
    )


def norm_back(grad_out, normal, inv_root, gain):
    scaled = grad_out * gain
    grad_gain = jnp.sum(grad_out * normal, 0)
    grad_in = inv_root * (scaled - normal * jnp.mean(scaled * normal, -1, keepdims=True))
    return (grad_in, grad_gain)


def pad_columns(values, width):
    return jnp.pad(values, ((0, 0), (0, width - values.shape[1])))


def up_to(value, step):
    return -(-value // step) * step


def hop(values, flip):
    return lax.ppermute(values, CTX, [(i, i ^ flip) for i in range(4)])


def by_part(pieces):
    own = lax.axis_index(CTX)
    low = (own & 1) == 1
    high = (own & 2) == 2
    first = [jnp.where(low, pieces[a ^ 1], pieces[a]) for a in range(4)]
    return [jnp.where(high, first[a ^ 2], first[a]) for a in range(4)]


def gather_ctx(values):
    half = values.shape[0] // 2
    one = hop(values, 1)
    two = hop(values, 2)
    return jnp.concatenate([values, one, two, hop(two[:half], 1), hop(one[half:], 2)], 0)


def scatter_ctx(values):
    tok = values.shape[0] // 4
    return scatter_pieces([values[j * tok : (j + 1) * tok] for j in range(4)])


def scatter_pieces(pieces):
    half = pieces[0].shape[0] // 2
    head = [piece[:half] for piece in pieces]
    tail = [piece[half:] for piece in pieces]
    head_pass = hop(head[3], 1)
    tail_pass = hop(tail[3], 2)
    head_own = hop(head[1], 1)
    tail_own = hop(tail[2], 2)
    head_next = (head[2].astype(F32) + head_pass.astype(F32)).astype(BF)
    tail_next = (tail[1].astype(F32) + tail_pass.astype(F32)).astype(BF)
    head_last = hop(head_next, 2)
    tail_last = hop(tail_next, 1)
    return jnp.concatenate(
        [
            head[0].astype(F32) + head_own.astype(F32) + head_last.astype(F32),
            tail[0].astype(F32) + tail_own.astype(F32) + tail_last.astype(F32),
        ],
        0,
    )


def gather_all(values):
    return lax.all_gather(values, ALL, axis=0, tiled=True)


def scatter_all(values):
    return lax.psum_scatter(values, ALL, scatter_dimension=0, tiled=True)


def swap_core(values):
    return lax.ppermute(values, "core", [(0, 1), (1, 0)])


def shift_chip(values, step):
    return lax.ppermute(values, "chip", [(i, (i + step) % 4) for i in range(4)])


def put(target, values, *place):
    return lax.dynamic_update_slice(target, values, place + (0,) * (target.ndim - len(place)))


def gather_line(values):
    chip = lax.axis_index("chip")
    line = jnp.zeros((4,) + values.shape, values.dtype)
    for step in range(4):
        piece = shift_chip(values, step) if step else values
        line = put(line, piece[None], (chip - step) % 4)
    return line


def gather_plane(line):
    one = hop(line, 1)
    two = hop(line, 2)
    return [line, one, two, hop(two[:2], 1), hop(one[2:], 2)]


def gather_cores(pieces):
    _, tok, width = pieces[0].shape
    part, _, core = (lax.axis_index(a) for a in ALL)
    full = jnp.zeros((4, 4, 2, tok, width), pieces[0].dtype)
    for piece, flip, first in zip(pieces, (0, 1, 2, 3, 3), (0, 0, 0, 0, 2)):
        other = swap_core(piece)
        full = put(full, piece[None, :, None], part ^ flip, first, core)
        full = put(full, other[None, :, None], part ^ flip, first, 1 - core)
    return full.reshape(-1, width)


def scatter_line(values, axis_values):
    chip = lax.axis_index("chip")
    total = lax.dynamic_index_in_dim(values, chip, 0, False)
    for step in range(1, 4):
        block = lax.dynamic_index_in_dim(axis_values, (chip + step) % 4, 0, False)
        total = total + shift_chip(block, step).astype(F32)
    return total


def add_cores(blocks):
    core = lax.axis_index("core")
    axis = blocks.ndim - 3
    away = swap_core(lax.dynamic_index_in_dim(blocks, 1 - core, axis, False))
    return lax.dynamic_index_in_dim(blocks, core, axis, False).astype(F32) + away.astype(F32)


def scatter_cores(values):
    part, _, core = (lax.axis_index(a) for a in ALL)
    tok = values[0].shape[0] // 32

    def rows(flip, side):
        return jnp.concatenate(
            [
                jnp.concatenate(
                    [
                        lax.dynamic_slice_in_dim(
                            value, (((part ^ flip) * 4 + chip) * 2 + side) * tok, tok, 0
                        )
                        for value in values
                    ],
                    1,
                )
                for chip in range(4)
            ],
            0,
        )

    away = [swap_core(rows(flip, 1 - core)) for flip in range(4)]
    return [
        (rows(flip, core).astype(F32) + away[flip].astype(F32)).astype(BF) for flip in range(4)
    ]


def scatter_rest(sums, beside):
    own, beside = lax.optimization_barrier((scatter_pieces(sums), beside))
    chip = lax.axis_index("chip")
    tok = own.shape[0] // 4
    total = lax.dynamic_slice_in_dim(own, chip * tok, tok, 0)
    low = own.astype(BF)
    for step in range(1, 4):
        block = lax.dynamic_slice_in_dim(low, (chip + step) % 4 * tok, tok, 0)
        total = total + shift_chip(block, step).astype(F32)
    return total, beside


def scatter_exp(values):
    if lax.axis_size("chip") != 4:
        return lax.psum_scatter(values, EXP, scatter_dimension=0, tiled=True).astype(F32)
    own = add_cores(values.reshape(4, 2, -1, values.shape[1]))
    return scatter_line(own, own.astype(BF))


def split_query(weight, parts):
    rows = weight.shape[0]
    heads = weight.reshape(rows, parts, HEADS // parts, NOPE + ROPE_D)
    half = NOPE + ROPE_D // 2
    return jnp.concatenate(
        [
            heads[..., :NOPE].reshape(rows, parts, -1),
            heads[..., NOPE:half].reshape(rows, parts, -1),
            heads[..., half:].reshape(rows, parts, -1),
        ],
        -1,
    )


def join_query(values, parts):
    rows = values.shape[0]
    own = HEADS // parts
    wide = own * NOPE
    narrow = own * (ROPE_D // 2)
    return jnp.concatenate(
        [
            values[..., :wide].reshape(rows, parts, own, NOPE),
            values[..., wide : wide + narrow].reshape(rows, parts, own, ROPE_D // 2),
            values[..., wide + narrow :].reshape(rows, parts, own, ROPE_D // 2),
        ],
        -1,
    ).reshape(rows, -1)


def split_up(weight, parts):
    rows = weight.shape[0]
    heads = weight.reshape(rows, parts, HEADS // parts, NOPE + VD)
    return jnp.concatenate(
        [heads[..., :NOPE].reshape(rows, parts, -1), heads[..., NOPE:].reshape(rows, parts, -1)], -1
    )


def join_up(values, parts):
    rows = values.shape[0]
    own = HEADS // parts
    return jnp.concatenate(
        [
            values[..., : own * NOPE].reshape(rows, parts, own, NOPE),
            values[..., own * NOPE :].reshape(rows, parts, own, VD),
        ],
        -1,
    ).reshape(rows, -1)


def swap_parts(pieces):
    ordered = by_part(pieces)
    return by_part([ordered[0]] + [hop(ordered[j], j) for j in range(1, 4)])


def gather_exp(pieces):
    full = lax.all_gather(jnp.stack(pieces), EXP, axis=1, tiled=True)
    return full.reshape(-1, full.shape[-1])


def to_heads(weight):
    return gather_exp(swap_parts([weight[:, j] for j in range(4)]))


def from_heads(grad, parts):
    experts = lax.axis_size(EXP)
    width = grad.shape[-1]
    full = grad.astype(BF).reshape(parts, experts, -1, width).transpose(1, 0, 2, 3)
    own = lax.psum_scatter(full.reshape(-1, width), EXP, scatter_dimension=0, tiled=True)
    own = own.reshape(parts, -1, width)
    return jnp.stack(swap_parts([own[a] for a in range(4)]), 1)


def shards(
    inputs,
    cotangent,
    expert_ids,
    attn_gain,
    query_weight,
    latent_down,
    latent_gain,
    latent_up,
    output_weight,
    ffn_gain,
    router_weight,
    shared_gate,
    shared_up,
    shared_down,
    expert_gate,
    expert_up,
    expert_down,
):
    parts = lax.axis_size(CTX)
    expert_devices = lax.axis_size(EXP)
    devices = parts * expert_devices
    my_part = lax.axis_index(CTX)
    my_expert = lax.axis_index(EXP)
    tok = inputs.shape[1]
    width = inputs.shape[2]
    group = tok * parts
    total = tok * devices
    rows = query_weight.shape[0]
    lat_rows = latent_gain.shape[0]
    expert_count = router_weight.shape[1]
    own_heads = HEADS // parts
    half = ROPE_D // 2
    low_width = KVR + ROPE_D
    attn_scale = 1.0 / math.sqrt(NOPE + ROPE_D)

    chosen = expert_ids[0]
    mask_own = jnp.sum(
        (chosen[:, :, None] == jnp.arange(expert_count)[None, None, :]).astype(F32), 1
    )
    mask_cols = tok * expert_count // rows
    pack_used = low_width + expert_count + 3
    pack = jnp.concatenate(
        [
            latent_down,
            router_weight,
            attn_gain[:, None],
            ffn_gain[:, None],
            jnp.pad(latent_gain, (0, rows - lat_rows))[:, None],
            mask_own.astype(BF).reshape(rows, mask_cols),
        ],
        1,
    )
    pack = pad_columns(pack, up_to(pack_used + mask_cols, 128))
    pack_full = gather_exp(by_part([pack] + [hop(pack, j) for j in range(1, 4)]))
    group_in = gather_ctx(inputs[0])
    weight_down = pack_full[:, :low_width]
    weight_router = pack_full[:, low_width : low_width + expert_count]
    gain_attn = pack_full[:, low_width + expert_count].astype(F32)
    gain_ffn = pack_full[:, low_width + expert_count + 1].astype(F32)
    gain_latent = (
        pack_full[:, low_width + expert_count + 2]
        .reshape(devices, rows)[:, :lat_rows]
        .reshape(KVR)
        .astype(F32)
    )
    mask = pack_full[:, pack_used : pack_used + mask_cols].reshape(total, expert_count).astype(F32)

    weight_query = to_heads(split_query(query_weight, parts))
    weight_up = to_heads(split_up(latent_up, parts))
    weight_output = lax.all_gather(output_weight, EXP, axis=0, tiled=True)
    own_shared = lax.all_to_all(
        jnp.concatenate(
            [w.reshape(rows, devices, 1, -1) for w in (shared_gate, shared_up)], 2
        ).reshape(rows, -1),
        ALL, split_axis=1, concat_axis=0, tiled=True,
    )
    own_sgate, own_sup = jnp.split(own_shared, 2, axis=1)
    chunks = max(1, total // 4096)

    early = chunks == 1 and lax.axis_size("chip") == 4

    group_rows = jnp.arange(group)
    place = place_of(my_part ^ (group_rows // tok), group_rows % tok, P_DEV * parts)
    allowed = place[None, :] <= place[:, None]
    cosine, sine = rotation(place, ROPE_D)
    cos_heads = jnp.tile(cosine, (1, own_heads))
    sin_heads = jnp.tile(sine, (1, own_heads))
    group_tokens = group_in.astype(F32)
    inv_root = lax.rsqrt(jnp.mean(group_tokens * group_tokens, -1, keepdims=True) + EPS)
    normed = (group_tokens * inv_root * gain_attn).astype(BF)
    if early:
        normed, cot_line = lax.optimization_barrier((normed, gather_line(cotangent[0])))
    query_raw = mm(normed, weight_query)
    wide = own_heads * NOPE
    narrow = own_heads * half
    query_nope = query_raw[:, :wide].astype(BF)
    query_first = query_raw[:, wide : wide + narrow]
    query_second = query_raw[:, wide + narrow :]
    turned_first = (query_first * cos_heads - query_second * sin_heads).astype(BF)
    turned_second = (query_first * sin_heads + query_second * cos_heads).astype(BF)
    query_rot = jnp.stack(
        [
            jnp.concatenate(
                [
                    query_nope[:, h * NOPE : (h + 1) * NOPE],
                    turned_first[:, h * half : (h + 1) * half],
                    turned_second[:, h * half : (h + 1) * half],
                ],
                1,
            )
            for h in range(own_heads)
        ]
    )
    latent_raw = mm(normed, weight_down)
    compressed = latent_raw[:, :KVR]
    latent_root = lax.rsqrt(jnp.mean(compressed * compressed, -1, keepdims=True) + EPS)
    latent_hat = compressed * latent_root
    latent_norm = (latent_hat * gain_latent).astype(BF)
    rope_first = latent_raw[:, KVR : KVR + half]
    rope_second = latent_raw[:, KVR + half :]
    key_rope = jnp.concatenate(
        [rope_first * cosine - rope_second * sine, rope_first * sine + rope_second * cosine], 1
    ).astype(BF)
    key_value = mm(latent_norm, weight_up).astype(BF)
    keys = jnp.stack(
        [
            jnp.concatenate([key_value[:, h * NOPE : (h + 1) * NOPE], key_rope], 1)
            for h in range(own_heads)
        ]
    )
    values = jnp.stack(
        [key_value[:, wide + h * VD : wide + (h + 1) * VD] for h in range(own_heads)]
    )
    scores = jnp.einsum("htd,hsd->hts", query_rot, keys, preferred_element_type=F32) * attn_scale
    scores = jnp.where(allowed[None], scores, -1e30)
    exp_scores = jnp.exp(scores - jnp.max(scores, -1, keepdims=True))
    probs = exp_scores / jnp.sum(exp_scores, -1, keepdims=True)
    weights_low = probs.astype(BF)
    attended = (
        jnp.einsum("hts,hsd->thd", weights_low, values, preferred_element_type=F32)
        .astype(BF)
        .reshape(group, own_heads * VD)
    )
    if early:
        attended, cot_pieces = lax.optimization_barrier((attended, gather_plane(cot_line)))
    projected = scatter_ctx(mm(attended, weight_output).astype(BF))
    tokens = inputs[0].astype(F32)
    hidden = tokens + projected
    inv_mid = lax.rsqrt(jnp.mean(hidden * hidden, -1, keepdims=True) + EPS)
    hidden_hat = hidden * inv_mid
    mixed = (hidden_hat * gain_ffn).astype(BF)

    exp_local, _, ff_own = expert_gate.shape
    routed = exp_local * ff_own
    own_units = routed + own_sgate.shape[1]
    weight_in = jnp.concatenate(
        [expert_gate[i] for i in range(exp_local)]
        + [own_sgate]
        + [expert_up[i] for i in range(exp_local)]
        + [own_sup, weight_router],
        1,
    )
    weight_out = jnp.concatenate([expert_down.reshape(routed, width), shared_down], 0)
    first_expert = my_expert * exp_local

    def run_units(all_mixed, all_cot, mask):
        count = all_mixed.shape[0]
        activations = mm(all_mixed, weight_in)
        gate_activation = activations[:, :own_units]
        up_activation = activations[:, own_units : 2 * own_units]
        probs_all = jax.nn.softmax(activations[:, 2 * own_units :], axis=-1)
        gates_local = lax.dynamic_slice(probs_all * mask, (0, first_expert), (count, exp_local))
        mask_local = lax.dynamic_slice(mask, (0, first_expert), (count, exp_local))
        gate_columns = jnp.concatenate(
            [jnp.broadcast_to(gates_local[:, i : i + 1], (count, ff_own)) for i in range(exp_local)]
            + [jnp.ones((count, own_units - routed), F32)],
            1,
        )
        sigma = jax.nn.sigmoid(gate_activation)
        gated = gate_activation * sigma
        unit = (gated * up_activation).astype(BF).astype(F32)
        scaled_unit = (unit * gate_columns).astype(BF)
        grad_unit_raw = mm_nt(all_cot, weight_out)
        grad_gate_terms = grad_unit_raw * unit
        grad_gates = (
            jnp.concatenate(
                [
                    jnp.sum(grad_gate_terms[:, i * ff_own : (i + 1) * ff_own], 1, keepdims=True)
                    for i in range(exp_local)
                ],
                1,
            )
            * mask_local
        )
        grad_probs_part = lax.dynamic_update_slice(
            jnp.zeros((count, up_to(expert_count, 128)), F32), grad_gates, (0, first_expert)
        ).astype(BF)
        grad_unit = grad_unit_raw * gate_columns
        grad_gate_act = (
            grad_unit * up_activation * sigma * (1.0 + gate_activation * (1.0 - sigma))
        ).astype(BF)
        grad_up_act = (grad_unit * gated).astype(BF)
        grad_acts = jnp.concatenate([grad_gate_act, grad_up_act], 1)
        grad_mixed_part = mm_nt(grad_acts, weight_in[:, : 2 * own_units]).astype(BF)
        line = lax.axis_size("chip") == 4
        if line:
            grad_mixed_part, scaled_unit = lax.optimization_barrier((grad_mixed_part, scaled_unit))
            sums = scatter_cores([grad_mixed_part, grad_probs_part])
        out_part = mm(scaled_unit, weight_out).astype(BF)
        if line:
            sums, out_part, all_mixed, all_cot = lax.optimization_barrier(
                (sums, out_part, all_mixed, all_cot)
            )
        pair_grads = tuple(
            mm_tn(all_mixed, grad[:, i * ff_own : (i + 1) * ff_own])
            for grad in (grad_gate_act, grad_up_act)
            for i in range(exp_local)
        )
        routed_grads = (pair_grads, mm_tn(scaled_unit, all_cot))
        shared_grads = mm_tn(
            all_mixed, jnp.concatenate([grad_gate_act[:, routed:], grad_up_act[:, routed:]], 1)
        ).astype(BF)
        if line:
            out_sums = scatter_cores([out_part])
            back, (out_sums, routed_grads, shared_grads) = scatter_rest(
                sums, (out_sums, routed_grads, shared_grads)
            )
            out_sum, _ = scatter_rest(out_sums, ())
        else:
            back = scatter_all(jnp.concatenate([grad_mixed_part, grad_probs_part], 1)).astype(F32)
            out_sum = scatter_all(out_part)
        weight_grads = (routed_grads[0], shared_grads, routed_grads[1])
        return out_sum, back, weight_grads

    mask_tokens = mask.reshape(devices, tok, expert_count)
    runs = []
    for i in range(chunks):
        span = slice(i * tok // chunks, (i + 1) * tok // chunks)
        own_mixed, own_cot = mixed[span], cotangent[0, span]
        if runs:
            own_mixed, own_cot, _ = lax.optimization_barrier((own_mixed, own_cot, runs[-1][:2]))
        runs.append(
            run_units(
                gather_all(own_mixed),
                gather_cores(cot_pieces) if early else gather_all(own_cot),
                mask_tokens[:, span].reshape(-1, expert_count),
            )
        )
    out_sum = jnp.concatenate([r[0] for r in runs], 0).astype(F32)
    back = jnp.concatenate([r[1] for r in runs], 0)
    pair_grads, grad_shared, grad_down_all = jax.tree.map(
        lambda *terms: sum(terms[1:], terms[0].astype(F32)), *[r[2] for r in runs]
    )
    expert_gate_total = jnp.stack(pair_grads[:exp_local])
    expert_up_total = jnp.stack(pair_grads[exp_local:])
    expert_down_total = grad_down_all[:routed].reshape(exp_local, ff_own, width)
    sum_sdown = grad_down_all[routed:]
    sum_shared = lax.all_to_all(
        grad_shared.astype(BF), ALL, split_axis=0, concat_axis=1, tiled=True
    )

    grad_probs = back[:, width : width + expert_count]
    router_probs = jax.nn.softmax(mm(mixed, weight_router), axis=-1)
    grad_logits = (
        router_probs * (grad_probs - jnp.sum(router_probs * grad_probs, -1, keepdims=True))
    ).astype(BF)
    grad_router = mm_tn(mixed, grad_logits)
    grad_mixed = back[:, :width] + mm_nt(grad_logits, weight_router)
    grad_mid, grad_gain_ffn = norm_back(grad_mixed, hidden_hat, inv_mid, gain_ffn)
    grad_hidden = cotangent[0].astype(F32) + grad_mid
    grad_proj = gather_ctx(grad_hidden.astype(BF))
    grad_output = mm_tn(attended, grad_proj).astype(BF)
    grad_att = mm_nt(grad_proj, weight_output).astype(BF)
    grad_att = jnp.stack([grad_att[:, h * VD : (h + 1) * VD] for h in range(own_heads)])
    grad_weights = jnp.einsum("htd,hsd->hts", grad_att, values, preferred_element_type=F32)
    grad_values = jnp.einsum("hts,htd->shd", weights_low, grad_att, preferred_element_type=F32)
    grad_scores = (
        probs * (grad_weights - jnp.sum(probs * grad_weights, -1, keepdims=True))
    ).astype(BF)
    grad_query = (
        jnp.einsum("hts,hsd->htd", grad_scores, keys, preferred_element_type=F32) * attn_scale
    )
    grad_keys = (
        jnp.einsum("hts,htd->hsd", grad_scores, query_rot, preferred_element_type=F32) * attn_scale
    )
    grad_first = jnp.concatenate(
        [grad_query[h, :, NOPE : NOPE + half] for h in range(own_heads)], 1
    )
    grad_second = jnp.concatenate([grad_query[h, :, NOPE + half :] for h in range(own_heads)], 1)
    grad_qraw = jnp.concatenate(
        [grad_query[h, :, :NOPE] for h in range(own_heads)]
        + [
            grad_first * cos_heads + grad_second * sin_heads,
            grad_second * cos_heads - grad_first * sin_heads,
        ],
        1,
    ).astype(BF)
    grad_kv = jnp.concatenate(
        [grad_keys[h, :, :NOPE] for h in range(own_heads)]
        + [grad_values.reshape(group, own_heads * VD)],
        1,
    ).astype(BF)
    grad_low = jnp.concatenate(
        [mm_nt(grad_kv, weight_up), jnp.sum(grad_keys[:, :, NOPE:], 0)], 1
    )
    grad_low, sum_shared = lax.optimization_barrier((grad_low, sum_shared))
    sum_shared = sum_shared.astype(F32).reshape(rows, devices, 2, -1)
    sum_sgate, sum_sup = (sum_shared[:, :, i].reshape(rows, -1) for i in range(2))
    grad_low = scatter_ctx(pad_columns(grad_low.astype(BF), up_to(low_width, 128)))
    grad_front = scatter_ctx(mm_nt(grad_qraw, weight_query).astype(BF))
    head_grads = (mm_tn(normed, grad_qraw).astype(BF), mm_tn(latent_norm, grad_kv).astype(BF))
    sum_output = lax.psum_scatter(
        grad_output, EXP, scatter_dimension=0, tiled=True
    ).astype(F32)
    sum_query = join_query(from_heads(head_grads[0], parts), parts).astype(F32)
    sum_up = join_up(from_heads(head_grads[1], parts), parts).astype(F32)

    def own(values):
        return values[:tok]

    cos_own, sin_own = own(cosine), own(sine)
    grad_comp, grad_gain_latent = norm_back(
        grad_low[:, :KVR], own(latent_hat), own(latent_root), gain_latent
    )
    rope_grad_first = grad_low[:, KVR : KVR + half]
    rope_grad_second = grad_low[:, KVR + half : low_width]
    grad_lraw = jnp.concatenate(
        [
            grad_comp,
            rope_grad_first * cos_own + rope_grad_second * sin_own,
            rope_grad_second * cos_own - rope_grad_first * sin_own,
        ],
        1,
    ).astype(BF)
    lraw_group = gather_ctx(pad_columns(grad_lraw, up_to(low_width, 128)))[:, :low_width]
    block_rows = width // parts
    normed_block = lax.dynamic_slice_in_dim(normed, my_part * block_rows, block_rows, 1)
    grad_down = mm_tn(normed_block, lraw_group)
    grad_normed = grad_front + mm_nt(grad_lraw, weight_down)
    inv_own = own(inv_root)
    grad_entry, grad_gain_attn = norm_back(grad_normed, tokens * inv_own, inv_own, gain_attn)
    grad_inputs = grad_hidden + grad_entry

    small = jnp.concatenate(
        [
            grad_router,
            grad_gain_attn[:, None],
            grad_gain_ffn[:, None],
            jnp.pad(
                grad_gain_latent.reshape(devices, lat_rows), ((0, 0), (0, rows - lat_rows))
            ).reshape(width, 1),
        ],
        1,
    )
    small = pad_columns(small, up_to(pack_used, 128) - low_width).reshape(parts, block_rows, -1)
    small = by_part([small[a] for a in range(parts)])
    small = small[0] + sum(hop(small[j].astype(BF), j).astype(F32) for j in range(1, parts))
    pack_sum = scatter_exp(jnp.concatenate([grad_down, small], 1).astype(BF))
    return (
        (hidden + out_sum).astype(BF)[None],
        grad_inputs[None],
        pack_sum[:, low_width + expert_count],
        sum_query,
        pack_sum[:, :low_width],
        pack_sum[:lat_rows, low_width + expert_count + 2],
        sum_up,
        sum_output,
        pack_sum[:, low_width + expert_count + 1],
        pack_sum[:, low_width : low_width + expert_count],
        sum_sgate,
        sum_sup,
        sum_sdown,
        expert_gate_total,
        expert_up_total,
        expert_down_total,
    )


def solution(mesh):
    context, experts = mesh.devices.shape
    split = Mesh(mesh.devices.reshape(context, experts // 2, 2), ALL)
    tokens = P(EXP, CTX, None)
    dense = P(ALL, None)
    gain = P(ALL)
    columns = P(EXP, None, CTX)
    down = P(EXP, CTX, None)
    in_specs = (
        tokens, tokens, tokens, gain, dense, dense, gain, dense, dense, gain, dense, dense, dense,
        dense, columns, columns, down,
    )
    out_specs = (
        tokens, tokens, gain, dense, dense, gain, dense, dense, gain, dense, dense, dense, dense,
        columns, columns, down,
    )
    return jax.shard_map(
        shards, mesh=split, in_specs=in_specs, out_specs=out_specs, check_vma=False
    )
```

profile of v0, /device:TPU:0, one launch (start us, length us, event | category | flops | bytes accessed | tf_op | source)
XLA Modules:
  0.0 1101.3 jit_solution(6184429412908005284)
XLA Ops:
  61.4 7.0 collective-permute-done.7
  70.3 19.0 %collective-permute-done.8 = bf16[128,2048]{1,0:T(8,128)(2,1)} collective-permute-done((bf16[128,2048]{1,0:T(8,128)(2,1)S(1)}, bf16[128,2048]{1,0:T(8,128)(2,1)}, u32[]{:S(2)}, u32[]{:S(2)}) %collective-permute-start.8) | collective-permute-done | bytes 524320 | tf_op jit(solution)/shard_map/ppermute | solution.py:124
  115.4 34.2 %all-gather.10.cloned.1.call-done = bf16[4,512,768]{2,1,0:T(8,128)(2,1)} async-done(((bf16[4,64,768]{2,1,0:T(8,128)(2,1)}), bf16[4,512,768]{2,1,0:T(8,128)(2,1)}) %all-gather.10.cloned.1.call-update) | async-done | bytes 3145744 | tf_op jit(solution)/shard_map/all_gather | solution.py:274
  165.0 16.5 %collective-permute-done.18 = bf16[2,128,2048]{2,1,0:T(8,128)(2,1)S(1)} collective-permute-done((bf16[2,128,2048]{2,1,0:T(8,128)(2,1)S(1)}, bf16[2,128,2048]{2,1,0:T(8,128)(2,1)S(1)}, u32[]{:S(2)}, u32[]{:S(2)}) %collective-permute-start.18) | collective-permute-done | bytes 1048608 | tf_op jit(solution)/shard_map/ppermute | solution.py:67
  233.3 32.3 %all-to-all-done = bf16[64,32,176]{2,0,1:T(8,128)(2,1)S(1)} async-done(((bf16[64,32,176]{2,0,1:T(8,128)(2,1)}), bf16[64,32,176]{2,0,1:T(8,128)(2,1)S(1)}, u32[]{:S(2)}, u32[]{:S(2)}) %all-to-all-start) | async-done | bytes 720928 | tf_op jit(solution)/shard_map/all_to_all | solution.py:362
  314.0 33.8 %all-gather.14.cloned.1.call-done = bf16[4096,2048]{1,0:T(8,128)(2,1)} async-done(((bf16[128,2048]{1,0:T(8,128)(2,1)}), bf16[4096,2048]{1,0:T(8,128)(2,1)}) %all-gather.14.cloned.1.call-update) | async-done | bytes 16777232 | tf_op jit(solution)/shard_map/all_gather | solution.py:112
  347.9 35.0 %fusion.122 = f32[4096,1600]{0,1:T(8,128)} fusion(bf16[4096,2048]{1,0:T(8,128)(2,1)} %all-gather.14.cloned.1.call-done, bf16[2048,1600]{0,1:T(8,128)(2,1)} %constant_dynamic-update-slice_fusion.7), kind=kOutput, calls=%fused_computation.568 | convolution fusion | flops 26843545600 | bytes 49545216 | tf_op jit(solution)/shard_map/dot_general | solution.py:27
  391.4 45.3 %multiply_convert_fusion.2 = (bf16[4096,792]{0,1:T(8,128)(2,1)}, bf16[4096,792]{0,1:T(8,128)(2,1)}, bf16[4096,792]{0,1:T(8,128)(2,1)}, bf16[4096,792]{0,1:T(8,128)(2,1)}, f32[4096,792]{0,1:T(8,128)}) fusion(f32[4096,1600]{0,1:T(8,128)} %fusion.122, f32[4096,352]{0,1:T(8,128)} %broadcast_in_dim.153, f32[4096,352]{0,1:T(8,128)} %broadcast_in_dim.151, ...), kind=kOutput, calls=%fused_computation.13 | convolution fusion | flops 13362167808 | bytes 96439392 | tf_op jit(solution)/shard_map/dot_general | solution.py:35
  436.7 38.0 %convolution_convert_fusion.1 = bf16[4096,2048]{1,0:T(8,128)(2,1)} fusion(bf16[2048,1584]{0,1:T(8,128)(2,1)} %get-tuple-element.425, bf16[4096,792]{0,1:T(8,128)(2,1)} %get-tuple-element.225, bf16[4096,792]{0,1:T(8,128)(2,1)} %get-tuple-element.224), kind=kOutput, calls=%fused_computation.4 | convolution fusion | flops 26609451008 | bytes 36241408 | tf_op jit(solution)/shard_map/dot_general | solution.py:35
  527.4 24.8 %convolution_convert_fusion = bf16[4096,2048]{1,0:T(8,128)(2,1)} fusion(bf16[4096,792]{0,1:T(8,128)(2,1)} %get-tuple-element.55, bf16[88,2048]{1,0:T(8,128)(2,1)} %param.30, bf16[704,2048]{1,0:T(8,128)(2,1)} %bitcast.433), kind=kOutput, calls=%fused_computation.3 | convolution fusion | flops 13302431744 | bytes 26509312 | tf_op jit(solution)/shard_map/dot_general | solution.py:27
  558.2 8.0 add_convert_fusion
  566.3 6.4 add_convert_fusion.1
  579.3 6.4 add_convert_fusion.3
  585.8 11.6 %fusion.11 = f32[2048,352]{0,1:T(8,128)} fusion(bf16[4096,2048]{1,0:T(8,128)(2,1)} %all-gather.14.cloned.1.call-done, bf16[4096,792]{0,1:T(8,128)(2,1)S(1)} %bitcast.418), kind=kOutput, calls=%fused_computation.45 | convolution fusion | flops 5905580032 | bytes 22544384 | tf_op jit(solution)/shard_map/dot_general | solution.py:31
  597.4 11.5 %fusion.13 = f32[2048,352]{0,1:T(8,128)} fusion(bf16[4096,2048]{1,0:T(8,128)(2,1)} %all-gather.14.cloned.1.call-done, bf16[4096,792]{0,1:T(8,128)(2,1)S(1)} %bitcast.418), kind=kOutput, calls=%fused_computation.47 | convolution fusion | flops 5905580032 | bytes 22544384 | tf_op jit(solution)/shard_map/dot_general | solution.py:31
  608.9 11.5 %fusion.15 = f32[2048,352]{0,1:T(8,128)} fusion(bf16[4096,2048]{1,0:T(8,128)(2,1)} %all-gather.14.cloned.1.call-done, bf16[4096,792]{0,1:T(8,128)(2,1)S(1)} %bitcast.416), kind=kOutput, calls=%fused_computation.49 | convolution fusion | flops 5905580032 | bytes 22544384 | tf_op jit(solution)/shard_map/dot_general | solution.py:31
  620.4 11.5 %fusion.17 = f32[2048,352]{0,1:T(8,128)} fusion(bf16[4096,2048]{1,0:T(8,128)(2,1)} %all-gather.14.cloned.1.call-done, bf16[4096,792]{0,1:T(8,128)(2,1)S(1)} %bitcast.416), kind=kOutput, calls=%fused_computation.51 | convolution fusion | flops 5905580032 | bytes 22544384 | tf_op jit(solution)/shard_map/dot_general | solution.py:31
  637.9 19.9 %fusion.123 = f32[792,2048]{1,0:T(8,128)} fusion(bf16[4096,792]{0,1:T(8,128)(2,1)} %get-tuple-element.55, bf16[4096,2048]{1,0:T(8,128)(2,1)} %bitcast.69), kind=kOutput, calls=%fused_computation.569 | convolution fusion | flops 13287555072 | bytes 29753344 | tf_op jit(solution)/shard_map/dot_general | solution.py:31
  663.4 10.1 convolution_convert_fusion.6
  674.9 13.4 %collective-permute-done.39 = bf16[256,2176]{1,0:T(8,128)(2,1)S(1)} collective-permute-done((bf16[256,2176]{1,0:T(8,128)(2,1)S(1)}, bf16[256,2176]{1,0:T(8,128)(2,1)S(1)}, u32[]{:S(2)}, u32[]{:S(2)}) %collective-permute-start.39) | collective-permute-done | bytes 1114144 | tf_op jit(solution)/shard_map/ppermute | solution.py:67
  703.0 13.9 %collective-permute-done.35 = bf16[256,2176]{1,0:T(8,128)(2,1)S(1)} collective-permute-done((bf16[256,2176]{1,0:T(8,128)(2,1)S(1)}, bf16[256,2176]{1,0:T(8,128)(2,1)S(1)}, u32[]{:S(2)}, u32[]{:S(2)}) %collective-permute-start.35) | collective-permute-done | bytes 1114144 | tf_op jit(solution)/shard_map/ppermute | solution.py:67
  717.8 21.7 %collective-permute-done.40 = bf16[256,2176]{1,0:T(8,128)(2,1)S(1)} collective-permute-done((bf16[256,2176]{1,0:T(8,128)(2,1)S(1)}, bf16[256,2176]{1,0:T(8,128)(2,1)S(1)}, u32[]{:S(2)}, u32[]{:S(2)}) %collective-permute-start.40) | collective-permute-done | bytes 1114144 | tf_op jit(solution)/shard_map/ppermute | solution.py:67
  751.1 10.9 collective-permute-done.54
  762.0 22.2 %collective-permute-done.55 = bf16[128,2176]{1,0:T(8,128)(2,1)} collective-permute-done((bf16[128,2176]{1,0:T(8,128)(2,1)}, bf16[128,2176]{1,0:T(8,128)(2,1)}, u32[]{:S(2)}, u32[]{:S(2)}) %collective-permute-start.55) | collective-permute-done | bytes 557088 | tf_op jit(solution)/shard_map/ppermute | solution.py:124
  792.3 10.3 collective-permute-done.58
  842.1 13.9 %all-to-all-start.1 = ((bf16[32,64,176]{2,1,0:T(8,128)(2,1)}), bf16[32,64,176]{2,1,0:T(8,128)(2,1)}, u32[]{:S(2)}, u32[]{:S(2)}) async-start(bf16[32,64,176]{2,1,0:T(8,128)(2,1)} %bitcast.381), calls=%async_computation.1 | async-start | bytes 2097152 | tf_op jit(solution)/shard_map/all_to_all | solution.py:549
  875.2 16.8 %collective-permute-done.46 = bf16[256,2048]{1,0:T(8,128)(2,1)S(1)} collective-permute-done((bf16[256,2048]{1,0:T(8,128)(2,1)}, bf16[256,2048]{1,0:T(8,128)(2,1)S(1)}, u32[]{:S(2)}, u32[]{:S(2)}) %collective-permute-start.46) | collective-permute-done | bytes 1048608 | tf_op jit(solution)/shard_map/ppermute | solution.py:67
  942.4 7.6 slice_reduce_fusion.2
  989.9 12.3 %collective-permute-done.47 = bf16[256,2048]{1,0:T(8,128)(2,1)S(1)} collective-permute-done((bf16[256,2048]{1,0:T(8,128)(2,1)S(1)}, bf16[256,2048]{1,0:T(8,128)(2,1)S(1)}, u32[]{:S(2)}, u32[]{:S(2)}) %collective-permute-start.47) | collective-permute-done | bytes 1048608 | tf_op jit(solution)/shard_map/ppermute | solution.py:67
  1020.3 22.5 %collective-permute-done.81 = bf16[64,640]{1,0:T(8,128)(2,1)S(1)} collective-permute-done((bf16[64,640]{1,0:T(8,128)(2,1)S(1)}, bf16[64,640]{1,0:T(8,128)(2,1)S(1)}, u32[]{:S(2)}, u32[]{:S(2)}) %collective-permute-start.81) | collective-permute-done | bytes 81952 | tf_op jit(solution)/shard_map/ppermute | solution.py:124
  1043.0 14.0 %collective-permute-done.82 = bf16[64,640]{1,0:T(8,128)(2,1)S(1)} collective-permute-done((bf16[64,640]{1,0:T(8,128)(2,1)S(1)}, bf16[64,640]{1,0:T(8,128)(2,1)S(1)}, u32[]{:S(2)}, u32[]{:S(2)}) %collective-permute-start.82) | collective-permute-done | bytes 81952 | tf_op jit(solution)/shard_map/ppermute | solution.py:124
  1063.6 15.0 %collective-permute-done.53 = bf16[128,2048]{1,0:T(8,128)(2,1)} collective-permute-done((bf16[128,2048]{1,0:T(8,128)(2,1)}, bf16[128,2048]{1,0:T(8,128)(2,1)}, u32[]{:S(2)}, u32[]{:S(2)}) %collective-permute-start.53) | collective-permute-done | bytes 524320 | tf_op jit(solution)/shard_map/ppermute | solution.py:124
  (874 shorter events, 505.9 us)
Async XLA Ops:
  7.2 88.6 %all-gather.6.cloned.1.call-start = ((), (), s32[]{:S(2)}) async-start(), calls=%async_computation.5 | async-start | bytes 2949120 | tf_op jit(solution)/shard_map/all_gather | solution.py:274
  22.1 89.1 %all-gather.8.cloned.1.call-start = ((), (), s32[]{:S(2)}) async-start(), calls=%async_computation.6 | async-start | bytes 1179648 | tf_op jit(solution)/shard_map/all_gather | solution.py:274
  30.5 119.1 %all-gather.10.cloned.1.call-start = ((), (), s32[]{:S(2)}) async-start(), calls=%async_computation.7 | async-start | bytes 3538944 | tf_op jit(solution)/shard_map/all_gather | solution.py:274
  40.7 144.5 %all-gather.12.cloned.1.call-start = ((), (), s32[]{:S(2)}) async-start(), calls=%async_computation.8 | async-start | bytes 2359296 | tf_op jit(solution)/shard_map/all_gather | solution.py:361
  42.4 46.9 %collective-permute-start.8 = (bf16[128,2048]{1,0:T(8,128)(2,1)S(1)}, bf16[128,2048]{1,0:T(8,128)(2,1)}, u32[]{:S(2)}, u32[]{:S(2)}) collective-permute-start(bf16[128,2048]{1,0:T(8,128)(2,1)S(1)} %bitcast.379), channel_id=1, source_target_pairs={{0,4},{2,6},{4,0},{6,2},{1,5},{3,7},{5,1},{7,3},{8,12},{10,14},{12... | collective-permute-start | bytes 1572872 | tf_op jit(solution)/shard_map/ppermute | solution.py:124
  45.0 46.2 %collective-permute-start.9 = (bf16[128,2048]{1,0:T(8,128)(2,1)S(1)}, bf16[128,2048]{1,0:T(8,128)(2,1)}, u32[]{:S(2)}, u32[]{:S(2)}) collective-permute-start(bf16[128,2048]{1,0:T(8,128)(2,1)S(1)} %bitcast.380), channel_id=1, source_target_pairs={{0,6},{2,0},{4,2},{6,4},{1,7},{3,1},{5,3},{7,5},{8,14},{10,8},{12,... | collective-permute-start | bytes 1572872 | tf_op jit(solution)/shard_map/ppermute | solution.py:124
  48.4 299.5 %all-gather.14.cloned.1.call-start = ((), (), s32[]{:S(2)}) async-start(), calls=%async_computation.9 | async-start | bytes 17301504 | tf_op jit(solution)/shard_map/all_gather | solution.py:112
  58.1 37.1 %collective-permute-start.2 = (bf16[64,2048]{1,0:T(8,128)(2,1)S(1)}, bf16[64,2048]{1,0:T(8,128)(2,1)S(1)}, u32[]{:S(2)}, u32[]{:S(2)}) collective-permute-start(bf16[64,2048]{1,0:T(8,128)(2,1)S(1)} %slice.738), channel_id=1, source_target_pairs={{0,8},{8,0},{16,24},{24,16},{1,9},{9,1},{17,25},{25,17},{2,10},{10... | collective-permute-start | bytes 786440 | tf_op jit(solution)/shard_map/ppermute | solution.py:67
  60.2 35.1 %collective-permute-start.3 = (bf16[64,2048]{1,0:T(8,128)(2,1)S(1)}, bf16[64,2048]{1,0:T(8,128)(2,1)S(1)}, u32[]{:S(2)}, u32[]{:S(2)}) collective-permute-start(bf16[64,2048]{1,0:T(8,128)(2,1)S(1)} %slice.739), channel_id=1, source_target_pairs={{0,16},{8,24},{16,0},{24,8},{1,17},{9,25},{17,1},{25,9},{2,18},{10... | collective-permute-start | bytes 786440 | tf_op jit(solution)/shard_map/ppermute | solution.py:67
  99.9 56.1 %collective-permute-start.17 = (bf16[4,128,2048]{2,1,0:T(8,128)(2,1)}, bf16[4,128,2048]{2,1,0:T(8,128)(2,1)S(1)}, u32[]{:S(2)}, u32[]{:S(2)}) collective-permute-start(bf16[4,128,2048]{2,1,0:T(8,128)(2,1)} %bitcast_dynamic-update-slice_fusion.18), channel_id=1, source_target_pairs={{0,16},{8,24},{16,0},{24,8},{1,17},{9,25},{17,1},{25,9},{2,18},{10... | collective-permute-start | bytes 6291464 | tf_op jit(solution)/shard_map/ppermute | solution.py:67
  101.4 56.2 %collective-permute-start.16 = (bf16[4,128,2048]{2,1,0:T(8,128)(2,1)}, bf16[4,128,2048]{2,1,0:T(8,128)(2,1)}, u32[]{:S(2)}, u32[]{:S(2)}) collective-permute-start(bf16[4,128,2048]{2,1,0:T(8,128)(2,1)} %bitcast_dynamic-update-slice_fusion.18), channel_id=1, source_target_pairs={{0,8},{8,0},{16,24},{24,16},{1,9},{9,1},{17,25},{25,17},{2,10},{10... | collective-permute-start | bytes 6291464 | tf_op jit(solution)/shard_map/ppermute | solution.py:67
  222.4 43.2 %all-to-all-start = ((bf16[64,32,176]{2,0,1:T(8,128)(2,1)}), bf16[64,32,176]{2,0,1:T(8,128)(2,1)S(1)}, u32[]{:S(2)}, u32[]{:S(2)}) async-start(bf16[64,32,176]{2,0,1:T(8,128)(2,1)} %all_to_all.28), calls=%async_computation | async-start | bytes 2097152 | tf_op jit(solution)/shard_map/all_to_all | solution.py:362
  227.4 831.8 %reduce-scatter.6.cloned.1.call-start = ((), (), s32[]{:S(2)}) async-start(), calls=%async_computation.11 | async-start | bytes 1179648 | tf_op jit(solution)/shard_map/reduce_scatter | solution.py:286
  512.3 45.8 %collective-permute-start.34 = (bf16[512,2176]{1,0:T(8,128)(2,1)}, bf16[512,2176]{1,0:T(8,128)(2,1)}, u32[]{:S(2)}, u32[]{:S(2)}) collective-permute-start(bf16[512,2176]{1,0:T(8,128)(2,1)} %maximum_maximum_fusion.4), channel_id=1, source_target_pairs={{0,1},{1,0},{2,3},{3,2},{4,5},{5,4},{6,7},{7,6},{8,9},{9,8},{10,11... | collective-permute-start | bytes 6684680 | tf_op jit(solution)/shard_map/ppermute | solution.py:120
  521.8 44.4 %collective-permute-start.33 = (bf16[512,2176]{1,0:T(8,128)(2,1)}, bf16[512,2176]{1,0:T(8,128)(2,1)S(1)}, u32[]{:S(2)}, u32[]{:S(2)}) collective-permute-start(bf16[512,2176]{1,0:T(8,128)(2,1)} %maximum_maximum_fusion.3), channel_id=1, source_target_pairs={{0,1},{1,0},{2,3},{3,2},{4,5},{5,4},{6,7},{7,6},{8,9},{9,8},{10,11... | collective-permute-start | bytes 6684680 | tf_op jit(solution)/shard_map/ppermute | solution.py:120
  526.8 45.9 %collective-permute-start.32 = (bf16[512,2176]{1,0:T(8,128)(2,1)S(1)}, bf16[512,2176]{1,0:T(8,128)(2,1)S(1)}, u32[]{:S(2)}, u32[]{:S(2)}) collective-permute-start(bf16[512,2176]{1,0:T(8,128)(2,1)S(1)} %maximum_maximum_fusion.2), channel_id=1, source_target_pairs={{0,1},{1,0},{2,3},{3,2},{4,5},{5,4},{6,7},{7,6},{8,9},{9,8},{10,11... | collective-permute-start | bytes 6684680 | tf_op jit(solution)/shard_map/ppermute | solution.py:120
  660.4 34.4 %collective-permute-start.42 = (bf16[512,2048]{1,0:T(8,128)(2,1)S(1)}, bf16[512,2048]{1,0:T(8,128)(2,1)S(1)}, u32[]{:S(2)}, u32[]{:S(2)}) collective-permute-start(bf16[512,2048]{1,0:T(8,128)(2,1)S(1)} %pad_maximum_fusion.6), channel_id=1, source_target_pairs={{0,1},{1,0},{2,3},{3,2},{4,5},{5,4},{6,7},{7,6},{8,9},{9,8},{10,11... | collective-permute-start | bytes 6291464 | tf_op jit(solution)/shard_map/ppermute | solution.py:120
  693.9 45.6 %collective-permute-start.40 = (bf16[256,2176]{1,0:T(8,128)(2,1)S(1)}, bf16[256,2176]{1,0:T(8,128)(2,1)S(1)}, u32[]{:S(2)}, u32[]{:S(2)}) collective-permute-start(bf16[256,2176]{1,0:T(8,128)(2,1)S(1)} %add_convert_fusion.8), channel_id=1, source_target_pairs={{0,8},{8,0},{16,24},{24,16},{1,9},{9,1},{17,25},{25,17},{2,10},{10... | collective-permute-start | bytes 3342344 | tf_op jit(solution)/shard_map/ppermute | solution.py:67
  694.8 46.0 %collective-permute-start.37 = (bf16[256,2176]{1,0:T(8,128)(2,1)S(1)}, bf16[256,2176]{1,0:T(8,128)(2,1)S(1)}, u32[]{:S(2)}, u32[]{:S(2)}) collective-permute-start(bf16[256,2176]{1,0:T(8,128)(2,1)S(1)} %add_convert_fusion.9), channel_id=1, source_target_pairs={{0,16},{8,24},{16,0},{24,8},{1,17},{9,25},{17,1},{25,9},{2,18},{10... | collective-permute-start | bytes 3342344 | tf_op jit(solution)/shard_map/ppermute | solution.py:67
  744.9 39.2 %collective-permute-start.55 = (bf16[128,2176]{1,0:T(8,128)(2,1)}, bf16[128,2176]{1,0:T(8,128)(2,1)}, u32[]{:S(2)}, u32[]{:S(2)}) collective-permute-start(bf16[128,2176]{1,0:T(8,128)(2,1)} %get-tuple-element.305), channel_id=1, source_target_pairs={{0,4},{2,6},{4,0},{6,2},{1,5},{3,7},{5,1},{7,3},{8,12},{10,14},{12... | collective-permute-start | bytes 1671176 | tf_op jit(solution)/shard_map/ppermute | solution.py:124
  746.4 37.8 %collective-permute-start.56 = (bf16[128,2176]{1,0:T(8,128)(2,1)S(1)}, bf16[128,2176]{1,0:T(8,128)(2,1)}, u32[]{:S(2)}, u32[]{:S(2)}) collective-permute-start(bf16[128,2176]{1,0:T(8,128)(2,1)S(1)} %get-tuple-element.304), channel_id=1, source_target_pairs={{0,6},{2,0},{4,2},{6,4},{1,7},{3,1},{5,3},{7,5},{8,14},{10,8},{12,... | collective-permute-start | bytes 1671176 | tf_op jit(solution)/shard_map/ppermute | solution.py:124
  820.0 262.9 %reduce-scatter.4.cloned.1.call-start = ((), (), s32[]{:S(2)}) async-start(), calls=%async_computation.10 | async-start | bytes 3538944 | tf_op jit(solution)/shard_map/reduce_scatter | solution.py:286
  829.9 42.7 %collective-permute-start.49 = (bf16[256,2048]{1,0:T(8,128)(2,1)}, bf16[256,2048]{1,0:T(8,128)(2,1)}, u32[]{:S(2)}, u32[]{:S(2)}) collective-permute-start(bf16[256,2048]{1,0:T(8,128)(2,1)} %get-tuple-element.322), channel_id=1, source_target_pairs={{0,16},{8,24},{16,0},{24,8},{1,17},{9,25},{17,1},{25,9},{2,18},{10... | collective-permute-start | bytes 3145736 | tf_op jit(solution)/shard_map/ppermute | solution.py:67
  842.1 53.2 %all-to-all-start.1 = ((bf16[32,64,176]{2,1,0:T(8,128)(2,1)}), bf16[32,64,176]{2,1,0:T(8,128)(2,1)}, u32[]{:S(2)}, u32[]{:S(2)}) async-start(bf16[32,64,176]{2,1,0:T(8,128)(2,1)} %bitcast.381), calls=%async_computation.1 | async-start | bytes 2097152 | tf_op jit(solution)/shard_map/all_to_all | solution.py:549
  856.0 232.6 %reduce-scatter.8.cloned.1.call-start = ((), (), s32[]{:S(2)}) async-start(), calls=%async_computation.12 | async-start | bytes 2359296 | tf_op jit(solution)/shard_map/reduce_scatter | solution.py:603
  856.2 35.7 %collective-permute-start.46 = (bf16[256,2048]{1,0:T(8,128)(2,1)}, bf16[256,2048]{1,0:T(8,128)(2,1)S(1)}, u32[]{:S(2)}, u32[]{:S(2)}) collective-permute-start(bf16[256,2048]{1,0:T(8,128)(2,1)} %get-tuple-element.321), channel_id=1, source_target_pairs={{0,8},{8,0},{16,24},{24,16},{1,9},{9,1},{17,25},{25,17},{2,10},{10... | collective-permute-start | bytes 3145736 | tf_op jit(solution)/shard_map/ppermute | solution.py:67
  933.5 44.8 %collective-permute-start.45 = (bf16[256,2048]{1,0:T(8,128)(2,1)}, bf16[256,2048]{1,0:T(8,128)(2,1)}, u32[]{:S(2)}, u32[]{:S(2)}) collective-permute-start(bf16[256,2048]{1,0:T(8,128)(2,1)} %slice.653), channel_id=1, source_target_pairs={{0,8},{8,0},{16,24},{24,16},{1,9},{9,1},{17,25},{25,17},{2,10},{10... | collective-permute-start | bytes 3145736 | tf_op jit(solution)/shard_map/ppermute | solution.py:67
  1012.8 49.4 %collective-permute-start.51 = (bf16[128,2048]{1,0:T(8,128)(2,1)}, bf16[128,2048]{1,0:T(8,128)(2,1)}, u32[]{:S(2)}, u32[]{:S(2)}) collective-permute-start(bf16[128,2048]{1,0:T(8,128)(2,1)} %get-tuple-element.316), channel_id=1, source_target_pairs={{0,2},{2,4},{4,6},{6,0},{1,3},{3,5},{5,7},{7,1},{8,10},{10,12},{12... | collective-permute-start | bytes 1572872 | tf_op jit(solution)/shard_map/ppermute | solution.py:124
  1013.4 50.2 %collective-permute-start.52 = (bf16[128,2048]{1,0:T(8,128)(2,1)}, bf16[128,2048]{1,0:T(8,128)(2,1)}, u32[]{:S(2)}, u32[]{:S(2)}) collective-permute-start(bf16[128,2048]{1,0:T(8,128)(2,1)} %get-tuple-element.318), channel_id=1, source_target_pairs={{0,4},{2,6},{4,0},{6,2},{1,5},{3,7},{5,1},{7,3},{8,12},{10,14},{12... | collective-permute-start | bytes 1572872 | tf_op jit(solution)/shard_map/ppermute | solution.py:124
  1017.4 39.6 %collective-permute-start.82 = (bf16[64,640]{1,0:T(8,128)(2,1)S(1)}, bf16[64,640]{1,0:T(8,128)(2,1)S(1)}, u32[]{:S(2)}, u32[]{:S(2)}) collective-permute-start(bf16[64,640]{1,0:T(8,128)(2,1)S(1)} %get-tuple-element.431), channel_id=1, source_target_pairs={{0,4},{2,6},{4,0},{6,2},{1,5},{3,7},{5,1},{7,3},{8,12},{10,14},{12... | collective-permute-start | bytes 245768 | tf_op jit(solution)/shard_map/ppermute | solution.py:124
  1018.5 38.5 %collective-permute-start.83 = (bf16[64,640]{1,0:T(8,128)(2,1)S(1)}, bf16[64,640]{1,0:T(8,128)(2,1)S(1)}, u32[]{:S(2)}, u32[]{:S(2)}) collective-permute-start(bf16[64,640]{1,0:T(8,128)(2,1)S(1)} %get-tuple-element.430), channel_id=1, source_target_pairs={{0,6},{2,0},{4,2},{6,4},{1,7},{3,1},{5,3},{7,5},{8,14},{10,8},{12,... | collective-permute-start | bytes 245768 | tf_op jit(solution)/shard_map/ppermute | solution.py:124
  1042.7 35.9 %collective-permute-start.53 = (bf16[128,2048]{1,0:T(8,128)(2,1)}, bf16[128,2048]{1,0:T(8,128)(2,1)}, u32[]{:S(2)}, u32[]{:S(2)}) collective-permute-start(bf16[128,2048]{1,0:T(8,128)(2,1)} %get-tuple-element.317), channel_id=1, source_target_pairs={{0,6},{2,0},{4,2},{6,4},{1,7},{3,1},{5,3},{7,5},{8,14},{10,8},{12,... | collective-permute-start | bytes 1572872 | tf_op jit(solution)/shard_map/ppermute | solution.py:124
  (260 other events, 3326.5 us)
Sparse Core Ops, SparseCore 0:
  22.2 62.5 all-gather.5
  87.0 22.5 all-gather.7
  111.8 37.7 all-gather.9
  151.1 28.0 all-gather.11
  217.1 130.7 all-gather.13
  820.1 42.7 reduce-scatter.5
  865.2 46.1 reduce-scatter.3
  928.1 37.0 reduce-scatter.7
where the time goes:
time: 1110 us; the launch traced here: 1100 us
  waiting for transfers between devices  380 us (34%)
  matrix products  261 us (24%)
  local copies, waits for them, and re-layouts  196 us (18%)
  other arithmetic  127 us (11%)
  starting transfers between devices  120 us (11%)
  between operations  17.9 us (2%)
    ppermute x64, waiting for transfers between devices, hop(): return lax.ppermute(values, CTX, [(i, i ^ flip) for i in range(4)])  168 us
    ppermute x12, waiting for transfers between devices, shift_chip(): return lax.ppermute(values, 'chip', [(i, (i + step) % 4) for i in range(4)])  111 us
    dot_general x7, matrix products, mm_nt(): lax.dot_general(left, right, (((1,), (1,)), ((), ())), preferred_element_...  95.6 us
    dot_general x11, matrix products, mm_tn(): lax.dot_general(left, right, (((0,), (0,)), ((), ())), preferred_element_...  85.7 us
    ppermute x64, starting transfers between devices, hop(): return lax.ppermute(values, CTX, [(i, i ^ flip) for i in range(4)])  75.2 us
    dot_general x7, matrix products, mm(): lax.dot_general(left, right, (((1,), (0,)), ((), ())), preferred_element_...  72.3 us
    convert_element_type x8, other arithmetic, scatter_cores(): (rows(flip, core).astype(F32) + away[flip].astype(F32)).astype(BF)  36.2 us
    all_gather x3, waiting for transfers between devices, gather_exp(): full = lax.all_gather(jnp.stack(pieces), EXP, axis=1, tiled=True)  34.2 us
  transfers between devices with their start and end apart: 100, of which 44 were waited for; matrix products, arithmetic and copies ran while one was open for 27% of the time, Pallas kernels for 0%

commit v1 on v0

--- a/solution.py
+++ b/solution.py
@@ -172,19 +172,13 @@
 
 def scatter_cores(values):
     part, _, core = (lax.axis_index(a) for a in ALL)
-    tok = values[0].shape[0] // 32
+    tok = values.shape[0] // 32
 
     def rows(flip, side):
         return jnp.concatenate(
             [
-                jnp.concatenate(
-                    [
-                        lax.dynamic_slice_in_dim(
-                            value, (((part ^ flip) * 4 + chip) * 2 + side) * tok, tok, 0
-                        )
-                        for value in values
-                    ],
-                    1,
+                lax.dynamic_slice_in_dim(
+                    values, (((part ^ flip) * 4 + chip) * 2 + side) * tok, tok, 0
                 )
                 for chip in range(4)
             ],
@@ -205,7 +199,8 @@
     low = own.astype(BF)
     for step in range(1, 4):
         block = lax.dynamic_slice_in_dim(low, (chip + step) % 4 * tok, tok, 0)
-        total = total + shift_chip(block, step).astype(F32)
+        moved = shift_chip(block, step)
+        total = total + moved.astype(F32)
     return total, beside
 
 
@@ -452,6 +447,14 @@
         1,
     )
     weight_out = jnp.concatenate([expert_down.reshape(routed, width), shared_down], 0)
+    carried = up_to(expert_count, 128)
+    weight_back = jnp.concatenate(
+        [
+            jnp.pad(weight_in[:, : 2 * own_units], ((0, 0), (0, carried))),
+            jnp.pad(jnp.eye(carried, dtype=BF), ((0, 0), (2 * own_units, 0))),
+        ],
+        0,
+    )
     first_expert = my_expert * exp_local
 
     def run_units(all_mixed, all_cot, mask):
@@ -484,19 +487,19 @@
             * mask_local
         )
         grad_probs_part = lax.dynamic_update_slice(
-            jnp.zeros((count, up_to(expert_count, 128)), F32), grad_gates, (0, first_expert)
+            jnp.zeros((count, carried), F32), grad_gates, (0, first_expert)
         ).astype(BF)
         grad_unit = grad_unit_raw * gate_columns
         grad_gate_act = (
             grad_unit * up_activation * sigma * (1.0 + gate_activation * (1.0 - sigma))
         ).astype(BF)
         grad_up_act = (grad_unit * gated).astype(BF)
-        grad_acts = jnp.concatenate([grad_gate_act, grad_up_act], 1)
-        grad_mixed_part = mm_nt(grad_acts, weight_in[:, : 2 * own_units]).astype(BF)
+        grad_acts = jnp.concatenate([grad_gate_act, grad_up_act, grad_probs_part], 1)
+        grad_mixed_part = mm_nt(grad_acts, weight_back).astype(BF)
         line = lax.axis_size("chip") == 4
         if line:
             grad_mixed_part, scaled_unit = lax.optimization_barrier((grad_mixed_part, scaled_unit))
-            sums = scatter_cores([grad_mixed_part, grad_probs_part])
+            sums = scatter_cores(grad_mixed_part)
         out_part = mm(scaled_unit, weight_out).astype(BF)
         if line:
             sums, out_part, all_mixed, all_cot = lax.optimization_barrier(
@@ -507,20 +510,24 @@
             for grad in (grad_gate_act, grad_up_act)
             for i in range(exp_local)
         )
-        routed_grads = (pair_grads, mm_tn(scaled_unit, all_cot))
+        routed_grads = (
+            pair_grads,
+            mm_tn(scaled_unit[:, :routed], all_cot),
+            mm_tn(scaled_unit[:, routed:], all_cot),
+        )
         shared_grads = mm_tn(
             all_mixed, jnp.concatenate([grad_gate_act[:, routed:], grad_up_act[:, routed:]], 1)
         ).astype(BF)
         if line:
-            out_sums = scatter_cores([out_part])
+            out_sums = scatter_cores(out_part)
             back, (out_sums, routed_grads, shared_grads) = scatter_rest(
                 sums, (out_sums, routed_grads, shared_grads)
             )
             out_sum, _ = scatter_rest(out_sums, ())
         else:
-            back = scatter_all(jnp.concatenate([grad_mixed_part, grad_probs_part], 1)).astype(F32)
+            back = scatter_all(grad_mixed_part).astype(F32)
             out_sum = scatter_all(out_part)
-        weight_grads = (routed_grads[0], shared_grads, routed_grads[1])
+        weight_grads = (*routed_grads, shared_grads)
         return out_sum, back, weight_grads
 
     mask_tokens = mask.reshape(devices, tok, expert_count)
@@ -539,15 +546,19 @@
         )
     out_sum = jnp.concatenate([r[0] for r in runs], 0).astype(F32)
     back = jnp.concatenate([r[1] for r in runs], 0)
-    pair_grads, grad_shared, grad_down_all = jax.tree.map(
+    pair_grads, grad_down, sum_sdown, grad_shared = jax.tree.map(
         lambda *terms: sum(terms[1:], terms[0].astype(F32)), *[r[2] for r in runs]
     )
     expert_gate_total = jnp.stack(pair_grads[:exp_local])
     expert_up_total = jnp.stack(pair_grads[exp_local:])
-    expert_down_total = grad_down_all[:routed].reshape(exp_local, ff_own, width)
-    sum_sdown = grad_down_all[routed:]
+    expert_down_total = grad_down.reshape(exp_local, ff_own, width)
     sum_shared = lax.all_to_all(
-        grad_shared.astype(BF), ALL, split_axis=0, concat_axis=1, tiled=True
+        grad_shared.astype(BF).reshape(devices, rows, -1), ALL, split_axis=0, concat_axis=0,
+        tiled=True,
+    )
+    sum_sgate, sum_sup = (
+        part.transpose(1, 0, 2).reshape(rows, -1).astype(F32)
+        for part in jnp.split(sum_shared, 2, axis=2)
     )
 
     grad_probs = back[:, width : width + expert_count]
@@ -594,9 +605,6 @@
     grad_low = jnp.concatenate(
         [mm_nt(grad_kv, weight_up), jnp.sum(grad_keys[:, :, NOPE:], 0)], 1
     )
-    grad_low, sum_shared = lax.optimization_barrier((grad_low, sum_shared))
-    sum_shared = sum_shared.astype(F32).reshape(rows, devices, 2, -1)
-    sum_sgate, sum_sup = (sum_shared[:, :, i].reshape(rows, -1) for i in range(2))
     grad_low = scatter_ctx(pad_columns(grad_low.astype(BF), up_to(low_width, 128)))
     grad_front = scatter_ctx(mm_nt(grad_qraw, weight_query).astype(BF))
     head_grads = (mm_tn(normed, grad_qraw).astype(BF), mm_tn(latent_norm, grad_kv).astype(BF))

time: 1110 us -> 1060 us (0.955)
  local copies, waits for them, and re-layouts: 196 us -> 164 us
  other arithmetic: 127 us -> 110 us
    convert_element_type x8, other arithmetic: 36.2 us -> 20.5 us  [scatter_cores(): (rows(flip, core).astype(F32) + away[flip].astype(F32)).astype(BF)]
    slice x3 -> x0, local copies, waits for them, and re-layouts: 15.6 us -> none  [the longest x1 7.6 us: shards(): sum_shared[:, :, i].reshape(rows, -1)]
    ppermute x64, waiting for transfers between devices: 168 us -> 184 us  [hop(): return lax.ppermute(values, CTX, [(i, i ^ flip) for i in range(4)])]
    concatenate x9 -> x8, other arithmetic: 23.5 us -> 12.9 us  [rows(): jnp.concatenate([lax.dynamic_slice_in_dim(values, (((part ^ flip) * 4 + c...]
    dot_general x11 -> x12, matrix products: 85.7 us -> 92.8 us  [mm_tn(): lax.dot_general(left, right, (((0,), (0,)), ((), ())), preferred_element_...]
    unnamed x416 -> x326, local copies, waits for them, and re-layouts: 34.2 us -> 33.9 us
  transfers between devices with their start and end apart: 100 -> 100, of which waited for: 44 -> 46; matrix products, arithmetic and copies ran while one was open for 27% -> 27% of each run, Pallas kernels for 0% -> 0%
where the time goes in v1:
time: 1060 us; the launch traced here: 1050 us
  waiting for transfers between devices  383 us (36%)
  matrix products  260 us (25%)
  local copies, waits for them, and re-layouts  164 us (15%)
  starting transfers between devices  117 us (11%)
  other arithmetic  110 us (10%)
  between operations  17.6 us (2%)
    ppermute x64, waiting for transfers between devices, hop(): return lax.ppermute(values, CTX, [(i, i ^ flip) for i in range(4)])  184 us
    ppermute x12, waiting for transfers between devices, shift_chip(): return lax.ppermute(values, 'chip', [(i, (i + step) % 4) for i in range(4)])  109 us
    dot_general x12, matrix products, mm_tn(): lax.dot_general(left, right, (((0,), (0,)), ((), ())), preferred_element_...  92.8 us
    dot_general x7, matrix products, mm_nt(): lax.dot_general(left, right, (((1,), (1,)), ((), ())), preferred_element_...  86.9 us
    ppermute x64, starting transfers between devices, hop(): return lax.ppermute(values, CTX, [(i, i ^ flip) for i in range(4)])  78.1 us
    dot_general x7, matrix products, mm(): lax.dot_general(left, right, (((1,), (0,)), ((), ())), preferred_element_...  72.7 us
    all_gather x3, waiting for transfers between devices, gather_exp(): full = lax.all_gather(jnp.stack(pieces), EXP, axis=1, tiled=True)  34.3 us
    unnamed x326, local copies, waits for them, and re-layouts  33.9 us
  transfers between devices with their start and end apart: 100, of which 46 were waited for; matrix products, arithmetic and copies ran while one was open for 27% of the time, Pallas kernels for 0%

profile of v1, /device:TPU:0, one launch (start us, length us, event | category | flops | bytes accessed | tf_op | source)
XLA Modules:
  0.0 1051.8 jit_solution(6014352077736344762)
XLA Ops:
  70.3 19.0 %collective-permute-done.8 = bf16[128,2048]{1,0:T(8,128)(2,1)} collective-permute-done((bf16[128,2048]{1,0:T(8,128)(2,1)S(1)}, bf16[128,2048]{1,0:T(8,128)(2,1)}, u32[]{:S(2)}, u32[]{:S(2)}) %collective-permute-start.8) | collective-permute-done | bytes 524320 | tf_op jit(solution)/shard_map/ppermute | solution.py:124
  115.4 34.3 %all-gather.10.cloned.1.call-done = bf16[4,512,768]{2,1,0:T(8,128)(2,1)} async-done(((bf16[4,64,768]{2,1,0:T(8,128)(2,1)}), bf16[4,512,768]{2,1,0:T(8,128)(2,1)}) %all-gather.10.cloned.1.call-update) | async-done | bytes 3145744 | tf_op jit(solution)/shard_map/all_gather | solution.py:269
  165.1 16.3 %collective-permute-done.18 = bf16[2,128,2048]{2,1,0:T(8,128)(2,1)S(1)} collective-permute-done((bf16[2,128,2048]{2,1,0:T(8,128)(2,1)S(1)}, bf16[2,128,2048]{2,1,0:T(8,128)(2,1)S(1)}, u32[]{:S(2)}, u32[]{:S(2)}) %collective-permute-start.18) | collective-permute-done | bytes 1048608 | tf_op jit(solution)/shard_map/ppermute | solution.py:67
  234.1 31.4 %all-to-all-done = bf16[64,32,176]{2,0,1:T(8,128)(2,1)S(1)} async-done(((bf16[64,32,176]{2,0,1:T(8,128)(2,1)}), bf16[64,32,176]{2,0,1:T(8,128)(2,1)S(1)}, u32[]{:S(2)}, u32[]{:S(2)}) %all-to-all-start) | async-done | bytes 720928 | tf_op jit(solution)/shard_map/all_to_all | solution.py:357
  287.2 16.4 %broadcast_in_dim.139 = bf16[4,4,2,128,2048]{4,3,2,1,0:T(8,128)(2,1)} broadcast(bf16[]{:T(256)} %constant.162.clone.1), dimensions={} | broadcast | bytes 16777218 | tf_op jit(solution)/shard_map/broadcast_in_dim | solution.py:149
  323.6 24.3 %all-gather.14.cloned.1.call-done = bf16[4096,2048]{1,0:T(8,128)(2,1)} async-done(((bf16[128,2048]{1,0:T(8,128)(2,1)}), bf16[4096,2048]{1,0:T(8,128)(2,1)}) %all-gather.14.cloned.1.call-update) | async-done | bytes 16777232 | tf_op jit(solution)/shard_map/all_gather | solution.py:112
  347.9 34.9 %fusion.142 = f32[4096,1600]{0,1:T(8,128)} fusion(bf16[4096,2048]{1,0:T(8,128)(2,1)} %all-gather.14.cloned.1.call-done, bf16[2048,1600]{0,1:T(8,128)(2,1)} %constant_dynamic-update-slice_fusion.7), kind=kOutput, calls=%fused_computation.550 | convolution fusion | flops 26843545600 | bytes 49545216 | tf_op jit(solution)/shard_map/dot_general | solution.py:27
  391.3 35.8 %multiply_convert_fusion.2 = (bf16[4096,792]{0,1:T(8,128)(2,1)}, bf16[4096,792]{0,1:T(8,128)(2,1)}, bf16[4096,792]{0,1:T(8,128)(2,1)}, bf16[4096,792]{0,1:T(8,128)(2,1)}, f32[4096,792]{0,1:T(8,128)}) fusion(f32[4096,1600]{0,1:T(8,128)} %fusion.142, f32[4096,352]{0,1:T(8,128)} %broadcast_in_dim.153, f32[4096,352]{0,1:T(8,128)} %broadcast_in_dim.151, ...), kind=kOutput, calls=%fused_computation.17 | convolution fusion | flops 13362167808 | bytes 96439392 | tf_op jit(solution)/shard_map/dot_general | solution.py:35
  427.1 7.6 convert_multiply_fusion.1
  435.8 41.5 %convolution_convert_fusion = bf16[4096,2176]{1,0:T(8,128)(2,1)} fusion(bf16[4096,128]{0,1:T(8,128)(2,1)S(1)} %fusion.87, bf16[4096,792]{0,1:T(8,128)(2,1)} %get-tuple-element.205, bf16[4096,792]{0,1:T(8,128)(2,1)} %get-tuple-element.204, bf16[2048,1584]{0,1:T(8,128)(2,1)} %get-tuple-element.373, bf16[128,1712]{0,1:T(8,128)(2,1)S(1)} %copy-done.90), kind=kOutput, calls=%fused_computation.1 | convolution fusion | flops 30591094784 | bytes 38776832 | tf_op jit(solution)/shard_map/dot_general | solution.py:35
  493.0 25.2 %convolution_convert_fusion.1 = bf16[4096,2048]{1,0:T(8,128)(2,1)} fusion(bf16[4096,792]{0,1:T(8,128)(2,1)} %get-tuple-element.54, bf16[88,2048]{1,0:T(8,128)(2,1)} %param.30, bf16[704,2048]{1,0:T(8,128)(2,1)} %bitcast.435), kind=kOutput, calls=%fused_computation.4 | convolution fusion | flops 13302431744 | bytes 26509312 | tf_op jit(solution)/shard_map/dot_general | solution.py:27
  537.1 9.6 fusion.54
  546.7 17.4 %fusion.15 = f32[704,2048]{1,0:T(8,128)} fusion(bf16[4096,2048]{1,0:T(8,128)(2,1)} %bitcast.69, bf16[4096,792]{0,1:T(8,128)(2,1)S(1)} %bitcast.411), kind=kOutput, calls=%fused_computation.28 | convolution fusion | flops 11811160064 | bytes 28311552 | tf_op jit(solution)/shard_map/dot_general | solution.py:31
  564.2 11.4 %fusion.22 = f32[2048,352]{0,1:T(8,128)} fusion(bf16[4096,2048]{1,0:T(8,128)(2,1)} %all-gather.14.cloned.1.call-done, bf16[4096,792]{0,1:T(8,128)(2,1)S(1)} %bitcast.419), kind=kOutput, calls=%fused_computation.56 | convolution fusion | flops 5905580032 | bytes 22544384 | tf_op jit(solution)/shard_map/dot_general | solution.py:31
  575.6 11.9 %fusion.24 = f32[2048,352]{0,1:T(8,128)} fusion(bf16[4096,2048]{1,0:T(8,128)(2,1)} %all-gather.14.cloned.1.call-done, bf16[4096,792]{0,1:T(8,128)(2,1)S(1)} %bitcast.419), kind=kOutput, calls=%fused_computation.58 | convolution fusion | flops 5905580032 | bytes 22544384 | tf_op jit(solution)/shard_map/dot_general | solution.py:31
  587.5 11.5 %fusion.26 = f32[2048,352]{0,1:T(8,128)} fusion(bf16[4096,2048]{1,0:T(8,128)(2,1)} %all-gather.14.cloned.1.call-done, bf16[4096,792]{0,1:T(8,128)(2,1)S(1)} %bitcast.417), kind=kOutput, calls=%fused_computation.60 | convolution fusion | flops 5905580032 | bytes 22544384 | tf_op jit(solution)/shard_map/dot_general | solution.py:31
  599.0 11.5 %fusion.28 = f32[2048,352]{0,1:T(8,128)} fusion(bf16[4096,2048]{1,0:T(8,128)(2,1)} %all-gather.14.cloned.1.call-done, bf16[4096,792]{0,1:T(8,128)(2,1)S(1)} %bitcast.417), kind=kOutput, calls=%fused_computation.62 | convolution fusion | flops 5905580032 | bytes 22544384 | tf_op jit(solution)/shard_map/dot_general | solution.py:31
  620.6 9.8 convolution_convert_fusion.6
  637.9 8.3 collective-permute-done.39
  647.7 11.5 %collective-permute-done.36 = bf16[256,2176]{1,0:T(8,128)(2,1)} collective-permute-done((bf16[256,2176]{1,0:T(8,128)(2,1)}, bf16[256,2176]{1,0:T(8,128)(2,1)}, u32[]{:S(2)}, u32[]{:S(2)}) %collective-permute-start.36) | collective-permute-done | bytes 1114144 | tf_op jit(solution)/shard_map/ppermute | solution.py:67
  672.9 13.8 %collective-permute-done.35 = bf16[256,2176]{1,0:T(8,128)(2,1)S(1)} collective-permute-done((bf16[256,2176]{1,0:T(8,128)(2,1)S(1)}, bf16[256,2176]{1,0:T(8,128)(2,1)S(1)}, u32[]{:S(2)}, u32[]{:S(2)}) %collective-permute-start.35) | collective-permute-done | bytes 1114144 | tf_op jit(solution)/shard_map/ppermute | solution.py:67
  688.8 20.4 %collective-permute-done.40 = bf16[256,2176]{1,0:T(8,128)(2,1)S(1)} collective-permute-done((bf16[256,2176]{1,0:T(8,128)(2,1)S(1)}, bf16[256,2176]{1,0:T(8,128)(2,1)S(1)}, u32[]{:S(2)}, u32[]{:S(2)}) %collective-permute-start.40) | collective-permute-done | bytes 1114144 | tf_op jit(solution)/shard_map/ppermute | solution.py:67
  722.1 10.5 collective-permute-done.54
  732.6 21.4 %collective-permute-done.55 = bf16[128,2176]{1,0:T(8,128)(2,1)} collective-permute-done((bf16[128,2176]{1,0:T(8,128)(2,1)}, bf16[128,2176]{1,0:T(8,128)(2,1)}, u32[]{:S(2)}, u32[]{:S(2)}) %collective-permute-start.55) | collective-permute-done | bytes 557088 | tf_op jit(solution)/shard_map/ppermute | solution.py:124
  765.2 10.8 %collective-permute-done.58 = bf16[128,2048]{1,0:T(8,128)(2,1)S(1)} collective-permute-done((bf16[128,2048]{1,0:T(8,128)(2,1)S(1)}, bf16[128,2048]{1,0:T(8,128)(2,1)S(1)}, u32[]{:S(2)}, u32[]{:S(2)}) %collective-permute-start.58) | collective-permute-done | bytes 524320 | tf_op jit(solution)/shard_map/ppermute | solution.py:67
  778.0 22.4 %collective-permute-done.59 = bf16[64,2048]{1,0:T(8,128)(2,1)S(1)} collective-permute-done((bf16[64,2048]{1,0:T(8,128)(2,1)S(1)}, bf16[64,2048]{1,0:T(8,128)(2,1)S(1)}, u32[]{:S(2)}, u32[]{:S(2)}) %collective-permute-start.59) | collective-permute-done | bytes 262176 | tf_op jit(solution)/shard_map/ppermute | solution.py:67
  828.3 13.8 %all-to-all-start.1 = ((bf16[32,64,176]{2,1,0:T(8,128)(2,1)}), bf16[32,64,176]{2,1,0:T(8,128)(2,1)S(1)}, u32[]{:S(2)}, u32[]{:S(2)}) async-start(bf16[32,64,176]{2,1,0:T(8,128)(2,1)} %bitcast.380), calls=%async_computation.4 | async-start | bytes 2097152 | tf_op jit(solution)/shard_map/all_to_all | solution.py:555
  907.0 15.2 %collective-permute-done.75 = bf16[64,640]{0,1:T(8,128)(2,1)} collective-permute-done((bf16[64,640]{0,1:T(8,128)(2,1)}, bf16[64,640]{0,1:T(8,128)(2,1)}, u32[]{:S(2)}, u32[]{:S(2)}) %collective-permute-start.75) | collective-permute-done | bytes 81952 | tf_op jit(solution)/shard_map/ppermute | solution.py:67
  940.1 9.3 collective-permute-done.50
  970.0 22.9 %collective-permute-done.81 = bf16[64,640]{1,0:T(8,128)(2,1)S(1)} collective-permute-done((bf16[64,640]{1,0:T(8,128)(2,1)S(1)}, bf16[64,640]{1,0:T(8,128)(2,1)S(1)}, u32[]{:S(2)}, u32[]{:S(2)}) %collective-permute-start.81) | collective-permute-done | bytes 81952 | tf_op jit(solution)/shard_map/ppermute | solution.py:124
  992.9 13.7 %collective-permute-done.82 = bf16[64,640]{1,0:T(8,128)(2,1)S(1)} collective-permute-done((bf16[64,640]{1,0:T(8,128)(2,1)S(1)}, bf16[64,640]{1,0:T(8,128)(2,1)S(1)}, u32[]{:S(2)}, u32[]{:S(2)}) %collective-permute-start.82) | collective-permute-done | bytes 81952 | tf_op jit(solution)/shard_map/ppermute | solution.py:124
  1013.2 14.9 %collective-permute-done.53 = bf16[128,2048]{1,0:T(8,128)(2,1)} collective-permute-done((bf16[128,2048]{1,0:T(8,128)(2,1)}, bf16[128,2048]{1,0:T(8,128)(2,1)}, u32[]{:S(2)}, u32[]{:S(2)}) %collective-permute-start.53) | collective-permute-done | bytes 524320 | tf_op jit(solution)/shard_map/ppermute | solution.py:124
  (780 shorter events, 455.2 us)
Async XLA Ops:
  7.2 88.6 %all-gather.6.cloned.1.call-start = ((), (), s32[]{:S(2)}) async-start(), calls=%async_computation.5 | async-start | bytes 2949120 | tf_op jit(solution)/shard_map/all_gather | solution.py:269
  22.1 89.0 %all-gather.8.cloned.1.call-start = ((), (), s32[]{:S(2)}) async-start(), calls=%async_computation.6 | async-start | bytes 1179648 | tf_op jit(solution)/shard_map/all_gather | solution.py:269
  30.5 119.1 %all-gather.10.cloned.1.call-start = ((), (), s32[]{:S(2)}) async-start(), calls=%async_computation.7 | async-start | bytes 3538944 | tf_op jit(solution)/shard_map/all_gather | solution.py:269
  40.7 144.5 %all-gather.12.cloned.1.call-start = ((), (), s32[]{:S(2)}) async-start(), calls=%async_computation.8 | async-start | bytes 2359296 | tf_op jit(solution)/shard_map/all_gather | solution.py:356
  42.4 46.9 %collective-permute-start.8 = (bf16[128,2048]{1,0:T(8,128)(2,1)S(1)}, bf16[128,2048]{1,0:T(8,128)(2,1)}, u32[]{:S(2)}, u32[]{:S(2)}) collective-permute-start(bf16[128,2048]{1,0:T(8,128)(2,1)S(1)} %bitcast.378), channel_id=1, source_target_pairs={{0,4},{2,6},{4,0},{6,2},{1,5},{3,7},{5,1},{7,3},{8,12},{10,14},{12... | collective-permute-start | bytes 1572872 | tf_op jit(solution)/shard_map/ppermute | solution.py:124
  45.0 46.2 %collective-permute-start.9 = (bf16[128,2048]{1,0:T(8,128)(2,1)S(1)}, bf16[128,2048]{1,0:T(8,128)(2,1)}, u32[]{:S(2)}, u32[]{:S(2)}) collective-permute-start(bf16[128,2048]{1,0:T(8,128)(2,1)S(1)} %bitcast.379), channel_id=1, source_target_pairs={{0,6},{2,0},{4,2},{6,4},{1,7},{3,1},{5,3},{7,5},{8,14},{10,8},{12,... | collective-permute-start | bytes 1572872 | tf_op jit(solution)/shard_map/ppermute | solution.py:124
  48.4 299.5 %all-gather.14.cloned.1.call-start = ((), (), s32[]{:S(2)}) async-start(), calls=%async_computation.9 | async-start | bytes 17301504 | tf_op jit(solution)/shard_map/all_gather | solution.py:112
  58.1 37.1 %collective-permute-start.2 = (bf16[64,2048]{1,0:T(8,128)(2,1)S(1)}, bf16[64,2048]{1,0:T(8,128)(2,1)S(1)}, u32[]{:S(2)}, u32[]{:S(2)}) collective-permute-start(bf16[64,2048]{1,0:T(8,128)(2,1)S(1)} %slice.730), channel_id=1, source_target_pairs={{0,8},{8,0},{16,24},{24,16},{1,9},{9,1},{17,25},{25,17},{2,10},{10... | collective-permute-start | bytes 786440 | tf_op jit(solution)/shard_map/ppermute | solution.py:67
  99.8 56.2 %collective-permute-start.17 = (bf16[4,128,2048]{2,1,0:T(8,128)(2,1)}, bf16[4,128,2048]{2,1,0:T(8,128)(2,1)S(1)}, u32[]{:S(2)}, u32[]{:S(2)}) collective-permute-start(bf16[4,128,2048]{2,1,0:T(8,128)(2,1)} %bitcast_dynamic-update-slice_fusion.18), channel_id=1, source_target_pairs={{0,16},{8,24},{16,0},{24,8},{1,17},{9,25},{17,1},{25,9},{2,18},{10... | collective-permute-start | bytes 6291464 | tf_op jit(solution)/shard_map/ppermute | solution.py:67
  101.3 56.3 %collective-permute-start.16 = (bf16[4,128,2048]{2,1,0:T(8,128)(2,1)}, bf16[4,128,2048]{2,1,0:T(8,128)(2,1)}, u32[]{:S(2)}, u32[]{:S(2)}) collective-permute-start(bf16[4,128,2048]{2,1,0:T(8,128)(2,1)} %bitcast_dynamic-update-slice_fusion.18), channel_id=1, source_target_pairs={{0,8},{8,0},{16,24},{24,16},{1,9},{9,1},{17,25},{25,17},{2,10},{10... | collective-permute-start | bytes 6291464 | tf_op jit(solution)/shard_map/ppermute | solution.py:67
  222.4 43.2 %all-to-all-start = ((bf16[64,32,176]{2,0,1:T(8,128)(2,1)}), bf16[64,32,176]{2,0,1:T(8,128)(2,1)S(1)}, u32[]{:S(2)}, u32[]{:S(2)}) async-start(bf16[64,32,176]{2,0,1:T(8,128)(2,1)} %all_to_all.17), calls=%async_computation | async-start | bytes 2097152 | tf_op jit(solution)/shard_map/all_to_all | solution.py:357
  227.4 781.4 %reduce-scatter.6.cloned.1.call-start = ((), (), s32[]{:S(2)}) async-start(), calls=%async_computation.11 | async-start | bytes 1179648 | tf_op jit(solution)/shard_map/reduce_scatter | solution.py:281
  270.7 36.1 %collective-permute-start.26 = (bf16[4,128,2048]{2,1,0:T(8,128)(2,1)}, bf16[4,128,2048]{2,1,0:T(8,128)(2,1)}, u32[]{:S(2)}, u32[]{:S(2)}) collective-permute-start(bf16[4,128,2048]{2,1,0:T(8,128)(2,1)} %bitcast_dynamic-update-slice_fusion.18), channel_id=1, source_target_pairs={{0,1},{1,0},{2,3},{3,2},{4,5},{5,4},{6,7},{7,6},{8,9},{9,8},{10,11... | collective-permute-start | bytes 6291464 | tf_op jit(solution)/shard_map/ppermute | solution.py:120
  287.2 35.4 %collective-permute-start.30 = (bf16[2,128,2048]{2,1,0:T(8,128)(2,1)S(1)}, bf16[2,128,2048]{2,1,0:T(8,128)(2,1)S(1)}, u32[]{:S(2)}, u32[]{:S(2)}) collective-permute-start(bf16[2,128,2048]{2,1,0:T(8,128)(2,1)S(1)} %copy-done.73), channel_id=1, source_target_pairs={{0,1},{1,0},{2,3},{3,2},{4,5},{5,4},{6,7},{7,6},{8,9},{9,8},{10,11... | collective-permute-start | bytes 3145736 | tf_op jit(solution)/shard_map/ppermute | solution.py:120
  483.6 40.6 %collective-permute-start.34 = (bf16[512,2176]{1,0:T(8,128)(2,1)}, bf16[512,2176]{1,0:T(8,128)(2,1)}, u32[]{:S(2)}, u32[]{:S(2)}) collective-permute-start(bf16[512,2176]{1,0:T(8,128)(2,1)} %pad_maximum_fusion.8), channel_id=1, source_target_pairs={{0,1},{1,0},{2,3},{3,2},{4,5},{5,4},{6,7},{7,6},{8,9},{9,8},{10,11... | collective-permute-start | bytes 6684680 | tf_op jit(solution)/shard_map/ppermute | solution.py:120
  485.5 42.3 %collective-permute-start.33 = (bf16[512,2176]{1,0:T(8,128)(2,1)}, bf16[512,2176]{1,0:T(8,128)(2,1)}, u32[]{:S(2)}, u32[]{:S(2)}) collective-permute-start(bf16[512,2176]{1,0:T(8,128)(2,1)} %pad_maximum_fusion.7), channel_id=1, source_target_pairs={{0,1},{1,0},{2,3},{3,2},{4,5},{5,4},{6,7},{7,6},{8,9},{9,8},{10,11... | collective-permute-start | bytes 6684680 | tf_op jit(solution)/shard_map/ppermute | solution.py:120
  492.7 38.8 %collective-permute-start.32 = (bf16[512,2176]{1,0:T(8,128)(2,1)}, bf16[512,2176]{1,0:T(8,128)(2,1)}, u32[]{:S(2)}, u32[]{:S(2)}) collective-permute-start(bf16[512,2176]{1,0:T(8,128)(2,1)} %pad_maximum_fusion.6), channel_id=1, source_target_pairs={{0,1},{1,0},{2,3},{3,2},{4,5},{5,4},{6,7},{7,6},{8,9},{9,8},{10,11... | collective-permute-start | bytes 6684680 | tf_op jit(solution)/shard_map/ppermute | solution.py:120
  617.3 44.0 %collective-permute-start.44 = (bf16[512,2048]{1,0:T(8,128)(2,1)}, bf16[512,2048]{1,0:T(8,128)(2,1)S(1)}, u32[]{:S(2)}, u32[]{:S(2)}) collective-permute-start(bf16[512,2048]{1,0:T(8,128)(2,1)} %pad_maximum_fusion.12), channel_id=1, source_target_pairs={{0,1},{1,0},{2,3},{3,2},{4,5},{5,4},{6,7},{7,6},{8,9},{9,8},{10,11... | collective-permute-start | bytes 6291464 | tf_op jit(solution)/shard_map/ppermute | solution.py:120
  663.7 45.6 %collective-permute-start.40 = (bf16[256,2176]{1,0:T(8,128)(2,1)S(1)}, bf16[256,2176]{1,0:T(8,128)(2,1)S(1)}, u32[]{:S(2)}, u32[]{:S(2)}) collective-permute-start(bf16[256,2176]{1,0:T(8,128)(2,1)S(1)} %add_convert_fusion.8), channel_id=1, source_target_pairs={{0,8},{8,0},{16,24},{24,16},{1,9},{9,1},{17,25},{25,17},{2,10},{10... | collective-permute-start | bytes 3342344 | tf_op jit(solution)/shard_map/ppermute | solution.py:67
  664.5 46.5 %collective-permute-start.37 = (bf16[256,2176]{1,0:T(8,128)(2,1)S(1)}, bf16[256,2176]{1,0:T(8,128)(2,1)S(1)}, u32[]{:S(2)}, u32[]{:S(2)}) collective-permute-start(bf16[256,2176]{1,0:T(8,128)(2,1)S(1)} %add_convert_fusion.9), channel_id=1, source_target_pairs={{0,16},{8,24},{16,0},{24,8},{1,17},{9,25},{17,1},{25,9},{2,18},{10... | collective-permute-start | bytes 3342344 | tf_op jit(solution)/shard_map/ppermute | solution.py:67
  715.5 38.5 %collective-permute-start.55 = (bf16[128,2176]{1,0:T(8,128)(2,1)}, bf16[128,2176]{1,0:T(8,128)(2,1)}, u32[]{:S(2)}, u32[]{:S(2)}) collective-permute-start(bf16[128,2176]{1,0:T(8,128)(2,1)} %get-tuple-element.285), channel_id=1, source_target_pairs={{0,4},{2,6},{4,0},{6,2},{1,5},{3,7},{5,1},{7,3},{8,12},{10,14},{12... | collective-permute-start | bytes 1671176 | tf_op jit(solution)/shard_map/ppermute | solution.py:124
  717.0 37.0 %collective-permute-start.56 = (bf16[128,2176]{1,0:T(8,128)(2,1)}, bf16[128,2176]{1,0:T(8,128)(2,1)}, u32[]{:S(2)}, u32[]{:S(2)}) collective-permute-start(bf16[128,2176]{1,0:T(8,128)(2,1)} %get-tuple-element.284), channel_id=1, source_target_pairs={{0,6},{2,0},{4,2},{6,4},{1,7},{3,1},{5,3},{7,5},{8,14},{10,8},{12,... | collective-permute-start | bytes 1671176 | tf_op jit(solution)/shard_map/ppermute | solution.py:124
  763.0 87.2 %collective-permute-start.49 = (bf16[256,2048]{1,0:T(8,128)(2,1)}, bf16[256,2048]{1,0:T(8,128)(2,1)}, u32[]{:S(2)}, u32[]{:S(2)}) collective-permute-start(bf16[256,2048]{1,0:T(8,128)(2,1)} %get-tuple-element.302), channel_id=1, source_target_pairs={{0,16},{8,24},{16,0},{24,8},{1,17},{9,25},{17,1},{25,9},{2,18},{10... | collective-permute-start | bytes 3145736 | tf_op jit(solution)/shard_map/ppermute | solution.py:67
  764.7 92.3 %collective-permute-start.46 = (bf16[256,2048]{1,0:T(8,128)(2,1)}, bf16[256,2048]{1,0:T(8,128)(2,1)}, u32[]{:S(2)}, u32[]{:S(2)}) collective-permute-start(bf16[256,2048]{1,0:T(8,128)(2,1)} %get-tuple-element.301), channel_id=1, source_target_pairs={{0,8},{8,0},{16,24},{24,16},{1,9},{9,1},{17,25},{25,17},{2,10},{10... | collective-permute-start | bytes 3145736 | tf_op jit(solution)/shard_map/ppermute | solution.py:67
  811.9 220.5 %reduce-scatter.4.cloned.1.call-start = ((), (), s32[]{:S(2)}) async-start(), calls=%async_computation.10 | async-start | bytes 3538944 | tf_op jit(solution)/shard_map/reduce_scatter | solution.py:281
  828.3 72.8 %all-to-all-start.1 = ((bf16[32,64,176]{2,1,0:T(8,128)(2,1)}), bf16[32,64,176]{2,1,0:T(8,128)(2,1)S(1)}, u32[]{:S(2)}, u32[]{:S(2)}) async-start(bf16[32,64,176]{2,1,0:T(8,128)(2,1)} %bitcast.380), calls=%async_computation.4 | async-start | bytes 2097152 | tf_op jit(solution)/shard_map/all_to_all | solution.py:555
  842.0 196.0 %reduce-scatter.8.cloned.1.call-start = ((), (), s32[]{:S(2)}) async-start(), calls=%async_computation.12 | async-start | bytes 2359296 | tf_op jit(solution)/shard_map/reduce_scatter | solution.py:611
  892.3 45.0 %collective-permute-start.45 = (bf16[256,2048]{1,0:T(8,128)(2,1)}, bf16[256,2048]{1,0:T(8,128)(2,1)}, u32[]{:S(2)}, u32[]{:S(2)}) collective-permute-start(bf16[256,2048]{1,0:T(8,128)(2,1)} %slice.649), channel_id=1, source_target_pairs={{0,8},{8,0},{16,24},{24,16},{1,9},{9,1},{17,25},{25,17},{2,10},{10... | collective-permute-start | bytes 3145736 | tf_op jit(solution)/shard_map/ppermute | solution.py:67
  962.9 49.2 %collective-permute-start.51 = (bf16[128,2048]{1,0:T(8,128)(2,1)}, bf16[128,2048]{1,0:T(8,128)(2,1)}, u32[]{:S(2)}, u32[]{:S(2)}) collective-permute-start(bf16[128,2048]{1,0:T(8,128)(2,1)} %get-tuple-element.296), channel_id=1, source_target_pairs={{0,2},{2,4},{4,6},{6,0},{1,3},{3,5},{5,7},{7,1},{8,10},{10,12},{12... | collective-permute-start | bytes 1572872 | tf_op jit(solution)/shard_map/ppermute | solution.py:124
  962.9 50.3 %collective-permute-start.52 = (bf16[128,2048]{1,0:T(8,128)(2,1)}, bf16[128,2048]{1,0:T(8,128)(2,1)}, u32[]{:S(2)}, u32[]{:S(2)}) collective-permute-start(bf16[128,2048]{1,0:T(8,128)(2,1)} %get-tuple-element.298), channel_id=1, source_target_pairs={{0,4},{2,6},{4,0},{6,2},{1,5},{3,7},{5,1},{7,3},{8,12},{10,14},{12... | collective-permute-start | bytes 1572872 | tf_op jit(solution)/shard_map/ppermute | solution.py:124
  967.6 39.1 %collective-permute-start.82 = (bf16[64,640]{1,0:T(8,128)(2,1)S(1)}, bf16[64,640]{1,0:T(8,128)(2,1)S(1)}, u32[]{:S(2)}, u32[]{:S(2)}) collective-permute-start(bf16[64,640]{1,0:T(8,128)(2,1)S(1)} %get-tuple-element.379), channel_id=1, source_target_pairs={{0,4},{2,6},{4,0},{6,2},{1,5},{3,7},{5,1},{7,3},{8,12},{10,14},{12... | collective-permute-start | bytes 245768 | tf_op jit(solution)/shard_map/ppermute | solution.py:124
  968.2 38.4 %collective-permute-start.83 = (bf16[64,640]{1,0:T(8,128)(2,1)S(1)}, bf16[64,640]{1,0:T(8,128)(2,1)S(1)}, u32[]{:S(2)}, u32[]{:S(2)}) collective-permute-start(bf16[64,640]{1,0:T(8,128)(2,1)S(1)} %get-tuple-element.378), channel_id=1, source_target_pairs={{0,6},{2,0},{4,2},{6,4},{1,7},{3,1},{5,3},{7,5},{8,14},{10,8},{12,... | collective-permute-start | bytes 245768 | tf_op jit(solution)/shard_map/ppermute | solution.py:124
  (215 other events, 2796.3 us)
Sparse Core Ops, SparseCore 0:
  22.2 62.5 all-gather.5
  87.0 22.6 all-gather.7
  111.9 37.6 all-gather.9
  151.1 28.0 all-gather.11
  217.1 130.7 all-gather.13
  812.0 43.3 reduce-scatter.5
  857.6 41.5 reduce-scatter.3
  901.5 37.8 reduce-scatter.7
